TPU v7x, 256 devices: a whole 4x4x8 slice. The times are simulated.
256 devices in a mesh: draw: 32 (over x, z), vocab: 8 (over y, core).
Axes of the slice: x: 4, y: 4, z: 8, core: 2. Of those that a mesh axis runs over, the one named last changes fastest.
Arguments:
- hidden: bfloat16 [64, 384, 896], P('draw'), may hold values from -256 to 256
- unembed: bfloat16 [896, 76032], P('draw', 'vocab'), may hold values from -1 to 1
- targets: int32 [384], replicated, may hold values from 0 to 76031
Outputs:
- influence: float32 [256, 128], P('draw')
All inputs are finite; a program needn't handle non-finite values.
Results may differ from a plain program's by a relative error of at most 0.0003.
Values may be sent and summed in bfloat16 or wider, within the bound.
No kernel may reach another device: no remote copies, remote signals or barrier semaphores. Data moves between devices by JAX's collectives and lax.ppermute only.
A program may use at most 192 MiB of HBM per device.

v0:
```python
import functools

import jax
import jax.numpy as jnp
from jax import lax
from jax.experimental import pallas as pl
from jax.experimental.pallas import tpu as pltpu
from jax.sharding import Mesh
from jax.sharding import PartitionSpec as P

TRAIN = 256
LANES = 128
WIDTHS = (1280, 1152)
WIDTH = sum(WIDTHS)
WIDEST = 512
CHUNK = 32


def shift(x, axis, by):
    size = lax.axis_size(axis)
    return lax.ppermute(x, axis, [(i, (i + by) % size) for i in range(size)])


def loss_kernel(place_ref, wanted_ref, *refs, sizes, counts, masked, merged):
    pieces = len(sizes)
    earlier_ref = refs[0] if merged else None
    refs = refs[1:] if merged else refs
    inputs = refs[:pieces]
    out_ref, held, weights, logits, top, total, picked, sems = refs[pieces:]
    tokens = wanted_ref.shape[0]
    rows_each = top.shape[0]
    blocks = held.shape[0] // rows_each
    copies, groups = [], []
    for count in counts:
        groups.append(range(len(copies), len(copies) + count))
        for k in groups[-1]:
            target = held if len(groups) > 1 else weights
            start = pl.multiple_of(place_ref[k], 16)
            copies.append(
                pltpu.make_async_copy(
                    inputs[k], target.at[pl.ds(start, sizes[k]), :], sems.at[k]
                )
            )
    for copy in copies:
        copy.start()
    limit = place_ref[pieces]
    width_all = weights.shape[1]
    tiles = [min(WIDEST, width_all - at) for at in range(0, width_all, WIDEST)]

    def product(slot, block, at, width):
        rows = held[pl.ds(pl.multiple_of(block * rows_each, 16), rows_each), :]
        logits[slot, :, :width] = jnp.dot(
            rows, weights[:, at : at + width], preferred_element_type=jnp.float32
        )

    def absorb(slot, at, width):
        for r in range(0, rows_each, CHUNK):
            some = slice(r, r + CHUNK)
            wanted = wanted_ref[r % tokens : r % tokens + CHUNK, :]
            chosen = picked[some, :] if at else jnp.zeros((CHUNK, LANES), jnp.float32)
            parts = []
            for g in range(0, width, LANES):
                part = logits[slot, some, g : g + LANES]
                chosen = jnp.where(wanted == at + g, part, chosen)
                if at + g >= width_all - masked:
                    lane = lax.broadcasted_iota(jnp.int32, part.shape, 1)
                    part = jnp.where(lane + (at + g) < limit, part, -jnp.inf)
                parts.append(part)
            high = parts[0]
            for part in parts[1:]:
                high = jnp.maximum(high, part)
            summed = jnp.zeros((CHUNK, LANES), jnp.float32)
            if at:
                before = top[some, :]
                high = jnp.maximum(high, before)
                summed = total[some, :] * jnp.exp(before - high)
            for part in parts:
                summed = summed + jnp.exp(part - high)
            top[some, :] = high
            total[some, :] = summed
            picked[some, :] = chosen

    def finish(block):
        for r in range(0, rows_each, LANES):
            some = slice(r, r + LANES)
            tops = jnp.transpose(top[some, :])
            totals = jnp.transpose(total[some, :])
            chosen = jnp.transpose(picked[some, :])
            high = jnp.max(tops, axis=0, keepdims=True)
            summed = jnp.sum(totals * jnp.exp(tops - high), axis=0, keepdims=True)
            chosen = jnp.sum(chosen, axis=0, keepdims=True)
            row = place_ref[pieces + 1 + block] + r // tokens
            at = slice(r % tokens, r % tokens + LANES)
            if merged:
                before = earlier_ref[0, row, :, at]
                joined = jnp.maximum(before, high)
                summed = summed * jnp.exp(high - joined) + jnp.exp(before - joined)
                high = joined
                chosen = chosen + earlier_ref[1, row, :, at]
            out_ref[0, row, :, at] = high + jnp.log(summed)
            out_ref[1, row, :, at] = chosen

    starts = [sum(tiles[:k]) for k in range(len(tiles))]
    last = (2, starts[-1], tiles[-1])

    def one_block(block, carry):
        for k, group in enumerate(groups[1:]):

            @pl.when(block == k)
            def _():
                for n in group:
                    copies[n].wait()

        product(0, block, starts[0], tiles[0])
        absorb(*last)
        finish(jnp.maximum(block - 1, 0))
        for step in range(1, len(tiles)):
            slot = 2 if step == len(tiles) - 1 else step % 2
            product(slot, block, starts[step], tiles[step])
            absorb((step - 1) % 2, starts[step - 1], tiles[step - 1])
        return carry

    for n in groups[0]:
        copies[n].wait()
    lax.fori_loop(0, blocks, one_block, 0)
    absorb(*last)
    finish(blocks - 1)


def local_stats(depth_pieces, row_blocks, spots, wanted, limit, masked, earlier=()):
    width = depth_pieces[0][0].shape[-1]
    depth = row_blocks[0][0][0].shape[-1]
    rows_each = sum(a.shape[0] for a, _ in row_blocks[0])
    blocks = len(row_blocks)
    groups = [list(depth_pieces)] + [
        [(a, k * rows_each + at) for a, at in block]
        for k, block in enumerate(row_blocks)
    ]
    everything = [piece for group in groups for piece in group]
    place = jnp.stack([jnp.asarray(s, jnp.int32) for _, s in everything] + [limit] + spots)
    pieces = [a for a, _ in everything]
    sizes = tuple(a.shape[0] for a in pieces)
    counts = tuple(len(group) for group in groups)
    state = pltpu.VMEM((rows_each, LANES), jnp.float32)
    return pl.pallas_call(
        functools.partial(
            loss_kernel, sizes=sizes, counts=counts, masked=masked, merged=len(earlier)
        ),
        out_shape=jax.ShapeDtypeStruct(
            (2, blocks * rows_each // wanted.shape[0], 1, wanted.shape[0]), jnp.float32
        ),
        in_specs=[
            pl.BlockSpec(memory_space=pltpu.SMEM),
            pl.BlockSpec(memory_space=pltpu.VMEM),
        ]
        + [pl.BlockSpec(memory_space=pltpu.VMEM)] * len(earlier)
        + [pl.BlockSpec(memory_space=pl.ANY)] * len(pieces),
        out_specs=pl.BlockSpec(memory_space=pltpu.VMEM),
        scratch_shapes=[
            pltpu.VMEM((blocks * rows_each, depth), jnp.bfloat16),
            pltpu.VMEM((depth, width), jnp.bfloat16),
            pltpu.VMEM((3, rows_each, WIDEST), jnp.float32),
            state,
            state,
            state,
            pltpu.SemaphoreType.DMA((len(pieces),)),
        ],
        compiler_params=pltpu.CompilerParams(vmem_limit_bytes=40 * 2**20),
        cost_estimate=pl.CostEstimate(
            flops=2 * blocks * rows_each * depth * width,
            bytes_accessed=2 * depth * (blocks * rows_each + width),
            transcendentals=blocks * rows_each * width,
        ),
    )(place, wanted, *earlier, *pieces)


def covariance(train_losses, query_losses):
    train_centered = train_losses - jnp.mean(train_losses, axis=0, keepdims=True)
    query_centered = query_losses - jnp.mean(query_losses, axis=0, keepdims=True)
    draw_count = train_losses.shape[0]
    return jnp.dot(
        train_centered.T,
        query_centered,
        precision=lax.Precision.HIGHEST,
        preferred_element_type=jnp.float32,
    ) / (draw_count - 1.0)


def body(hidden, unembed, targets):
    draws, tokens, model_width = hidden.shape
    depth_each, columns = unembed.shape
    nx, nz = lax.axis_size("x"), lax.axis_size("z")
    ny, nc = lax.axis_size("y"), lax.axis_size("c")
    x, z, y, c = (lax.axis_index(name) for name in ("x", "z", "y", "c"))

    padded = jnp.pad(unembed, ((0, 0), (0, nx * WIDTH - columns)))
    blocks = jnp.stack([padded[:, k * WIDTH : (k + 1) * WIDTH] for k in range(nx)])
    own = lax.all_to_all(blocks, "x", 0, 0, tiled=True)
    span = nx * depth_each
    depth_pieces = []
    for half, (at, width) in enumerate(((0, WIDTHS[0]), (WIDTHS[0], WIDTHS[1]))):
        part = own[:, :, at : at + width].reshape(span, width)
        found = [(part, z * span)]
        up = down = part
        for k in range(1, nz // 2):
            up = shift(up, "z", 1)
            down = shift(down, "z", -1)
            found.append((up, (z + nz - k) % nz * span))
            found.append((down, (z + k) % nz * span))
        far = (up, 1) if not half else (down, -1)
        far = shift(far[0], "z", far[1])
        found.append((far, (z + nz // 2) % nz * span))
        depth_pieces.append(found)

    source = jnp.arange(model_width, dtype=jnp.int32)
    zp, rest = source // span, source % span
    source = (rest // depth_each * nz + zp) * depth_each + rest % depth_each
    chooser = (
        lax.broadcasted_iota(jnp.int32, (model_width, model_width), 0)
        == source[None, :]
    ).astype(jnp.bfloat16)
    ordered = jnp.dot(
        hidden.reshape(draws * tokens, model_width),
        chooser,
        preferred_element_type=jnp.float32,
    ).astype(jnp.bfloat16)
    mine = lax.dynamic_slice_in_dim(ordered, c * tokens, tokens, 0)
    mine, _ = lax.optimization_barrier((mine, own))
    left, right = shift(mine, "x", 1), shift(mine, "x", -1)
    row_blocks = [[(ordered, 0)]]
    for rows in (left, right, shift(left, "x", 1)):
        row_blocks.append([(rows, c * tokens), (shift(rows, "c", 1), (1 - c) * tokens)])
    spots = [(x + k) % nx * draws for k in (0, nx - 1, 1, 2)]

    first_column = (y * nc + c) * columns + x * WIDTH
    wanted = (
        targets[:, None]
        - first_column
        - lax.broadcasted_iota(jnp.int32, (tokens, LANES), 1)
    )
    limit = jnp.minimum(columns - x * WIDTH, WIDTH).astype(jnp.int32)
    first = local_stats(depth_pieces[0], row_blocks, spots, wanted, limit, 0)
    stats = local_stats(
        depth_pieces[1],
        row_blocks,
        spots,
        wanted - WIDTHS[0],
        limit - WIDTHS[0],
        256,
        (first,),
    )[:, :, 0]

    sent = jnp.stack(
        [
            jnp.concatenate([stats[:, :, at : at + LANES], stats[:, :, TRAIN:]], axis=-1)
            for at in range(0, TRAIN, LANES)
        ]
    )
    sent = jnp.broadcast_to(
        sent[:, None], (len(sent), nx // len(sent) * ny * nc, *sent.shape[1:])
    )
    sent = sent.reshape(nx * ny * nc, *sent.shape[2:])
    got = lax.all_to_all(sent, ("x", "y", "c"), 0, 0, tiled=True)
    high = jnp.max(got[:, 0], axis=0)
    losses = (
        high
        + jnp.log(jnp.sum(jnp.exp(got[:, 0] - high[None]), axis=0))
        - jnp.sum(got[:, 1], axis=0)
    )
    got = lax.all_to_all(
        jnp.broadcast_to(losses[None], (nz, *losses.shape)), "z", 0, 0, tiled=True
    )
    got = got.reshape(-1, got.shape[-1])
    each = TRAIN // (nx * nz)
    mine = lax.dynamic_slice_in_dim(got, (x * nz + z) * each % LANES, each, 1)
    return covariance(mine, got[:, LANES:])


def solution(mesh):
    split = Mesh(mesh.devices.reshape(4, 8, 4, 2), ("x", "z", "y", "c"))
    draw, vocab = ("x", "z"), ("y", "c")
    placed = (P(draw, None, None), P(draw, vocab), P())
    return jax.shard_map(
        body, mesh=split, in_specs=placed, out_specs=P(draw, None), check_vma=False
    )
```

profile of v0, /device:TPU:1, one launch (start us, length us, event | category | flops | bytes accessed | tf_op | source)
XLA Modules:
  0.0 146.2 jit_solution(12798810794566704646)
XLA Ops:
  2.3 4.8 %all-to-all-start = ((bf16[4,28,2432]{2,1,0:T(8,128)(2,1)}), bf16[4,28,2432]{2,1,0:T(8,128)(2,1)}, u32[]{:S(2)}, u32[]{:S(2)}) async-start(bf16[4,28,2432]{2,1,0:T(8,128)(2,1)} %pad_maximum_fusion), calls=%async_computation | async-start | bytes 1245184 | tf_op jit(solution)/shard_map/all_to_all | solution.py:198
  7.1 1.8 %fusion.1 = bf16[896,768]{0,1:T(8,128)(2,1)S(1)} fusion(bf16[768,896]{1,0:T(8,128)(2,1)S(1)} %bitcast.48, s32[896]{0:T(1024)S(1)} %fusion.20), kind=kOutput, calls=%fused_computation.2 | convolution fusion | flops 1234616320 | bytes 2756096 | tf_op jit(solution)/shard_map/dot_general | solution.py:222
  9.9 5.2 %all-to-all-done = bf16[4,28,2432]{2,1,0:T(8,128)(2,1)} async-done(((bf16[4,28,2432]{2,1,0:T(8,128)(2,1)}), bf16[4,28,2432]{2,1,0:T(8,128)(2,1)}, u32[]{:S(2)}, u32[]{:S(2)}) %all-to-all-start) | async-done | bytes 544800 | tf_op jit(solution)/shard_map/all_to_all | solution.py:198
  16.4 3.8 %collective-permute-start.13 = (bf16[112,1152]{1,0:T(8,128)(2,1)S(1)}, bf16[112,1152]{1,0:T(8,128)(2,1)S(1)}, u32[]{:S(2)}, u32[]{:S(2)}) collective-permute-start(bf16[112,1152]{1,0:T(8,128)(2,1)S(1)} %reshape.71.refs_1_), channel_id=1, source_target_pairs={{0,8},{8,16},{16,24},{24,32},{32,40},{40,48},{48,56},{56,0},{1,9},... | collective-permute-start | bytes 774152 | tf_op jit(solution)/shard_map/ppermute | solution.py:21
  20.2 4.0 %collective-permute-start.14 = (bf16[112,1152]{1,0:T(8,128)(2,1)S(1)}, bf16[112,1152]{1,0:T(8,128)(2,1)}, u32[]{:S(2)}, u32[]{:S(2)}) collective-permute-start(bf16[112,1152]{1,0:T(8,128)(2,1)S(1)} %reshape.71.refs_1_), channel_id=1, source_target_pairs={{0,56},{8,0},{16,8},{24,16},{32,24},{40,32},{48,40},{56,48},{1,57}... | collective-permute-start | bytes 774152 | tf_op jit(solution)/shard_map/ppermute | solution.py:21
  24.2 2.4 %collective-permute-start.9 = (bf16[384,896]{1,0:T(8,128)(2,1)}, bf16[384,896]{1,0:T(8,128)(2,1)}, u32[]{:S(2)}, u32[]{:S(2)}) collective-permute-start(bf16[384,896]{1,0:T(8,128)(2,1)} %dynamic-slice_bitcast_fusion), channel_id=1, source_target_pairs={{0,192},{64,0},{128,64},{192,128},{1,193},{65,1},{129,65},{193,129... | collective-permute-start | bytes 2064392 | tf_op jit(solution)/shard_map/ppermute | solution.py:21
  26.6 3.3 %collective-permute-done.7.refs_9_.refs_10_ = bf16[384,896]{1,0:T(8,128)(2,1)} collective-permute-done((bf16[384,896]{1,0:T(8,128)(2,1)}, bf16[384,896]{1,0:T(8,128)(2,1)}, u32[]{:S(2)}, u32[]{:S(2)}) %collective-permute-start.7) | collective-permute-done | bytes 688160 | tf_op jit(solution)/shard_map/ppermute | solution.py:21
  29.9 1.7 %slice.51 = bf16[4,28,1280]{2,1,0:T(8,128)(2,1)} slice(bf16[4,28,2432]{2,1,0:T(8,128)(2,1)} %all-to-all-done), slice={[0:4], [0:28], [0:1280]} | slice | bytes 573440 | tf_op jit(solution)/shard_map/slice | solution.py:202
  32.7 5.7 %collective-permute-start = (bf16[112,1280]{1,0:T(8,128)(2,1)S(1)}, bf16[112,1280]{1,0:T(8,128)(2,1)S(1)}, u32[]{:S(2)}, u32[]{:S(2)}) collective-permute-start(bf16[112,1280]{1,0:T(8,128)(2,1)S(1)} %reshape.69.refs_0_), channel_id=1, source_target_pairs={{0,8},{8,16},{16,24},{24,32},{32,40},{40,48},{48,56},{56,0},{1,9},... | collective-permute-start | bytes 860168 | tf_op jit(solution)/shard_map/ppermute | solution.py:21
  38.4 4.0 %collective-permute-start.1 = (bf16[112,1280]{1,0:T(8,128)(2,1)S(1)}, bf16[112,1280]{1,0:T(8,128)(2,1)S(1)}, u32[]{:S(2)}, u32[]{:S(2)}) collective-permute-start(bf16[112,1280]{1,0:T(8,128)(2,1)S(1)} %reshape.69.refs_0_), channel_id=1, source_target_pairs={{0,56},{8,0},{16,8},{24,16},{32,24},{40,32},{48,40},{56,48},{1,57}... | collective-permute-start | bytes 860168 | tf_op jit(solution)/shard_map/ppermute | solution.py:21
  43.2 4.0 %collective-permute-done.refs_1_ = bf16[112,1280]{1,0:T(8,128)(2,1)S(1)} collective-permute-done((bf16[112,1280]{1,0:T(8,128)(2,1)S(1)}, bf16[112,1280]{1,0:T(8,128)(2,1)S(1)}, u32[]{:S(2)}, u32[]{:S(2)}) %collective-permute-start) | collective-permute-done | bytes 286752 | tf_op jit(solution)/shard_map/ppermute | solution.py:21
  47.9 2.7 %collective-permute-start.16 = (bf16[112,1152]{1,0:T(8,128)(2,1)}, bf16[112,1152]{1,0:T(8,128)(2,1)}, u32[]{:S(2)}, u32[]{:S(2)}) collective-permute-start(bf16[112,1152]{1,0:T(8,128)(2,1)} %collective-permute-done.14.refs_3_), channel_id=1, source_target_pairs={{0,56},{8,0},{16,8},{24,16},{32,24},{40,32},{48,40},{56,48},{1,57}... | collective-permute-start | bytes 774152 | tf_op jit(solution)/shard_map/ppermute | solution.py:21
  50.5 2.1 %collective-permute-done.15.refs_4_ = bf16[112,1152]{1,0:T(8,128)(2,1)} collective-permute-done((bf16[112,1152]{1,0:T(8,128)(2,1)S(1)}, bf16[112,1152]{1,0:T(8,128)(2,1)}, u32[]{:S(2)}, u32[]{:S(2)}) %collective-permute-start.15) | collective-permute-done | bytes 258080 | tf_op jit(solution)/shard_map/ppermute | solution.py:21
  54.6 4.2 %collective-permute-done.2.refs_3_ = bf16[112,1280]{1,0:T(8,128)(2,1)} collective-permute-done((bf16[112,1280]{1,0:T(8,128)(2,1)S(1)}, bf16[112,1280]{1,0:T(8,128)(2,1)}, u32[]{:S(2)}, u32[]{:S(2)}) %collective-permute-start.2) | collective-permute-done | bytes 286752 | tf_op jit(solution)/shard_map/ppermute | solution.py:21
  58.8 2.7 %collective-permute-start.18 = (bf16[112,1152]{1,0:T(8,128)(2,1)}, bf16[112,1152]{1,0:T(8,128)(2,1)S(1)}, u32[]{:S(2)}, u32[]{:S(2)}) collective-permute-start(bf16[112,1152]{1,0:T(8,128)(2,1)} %collective-permute-done.16.refs_5_), channel_id=1, source_target_pairs={{0,56},{8,0},{16,8},{24,16},{32,24},{40,32},{48,40},{56,48},{1,57}... | collective-permute-start | bytes 774152 | tf_op jit(solution)/shard_map/ppermute | solution.py:21
  62.2 6.4 %collective-permute-start.8 = (bf16[384,896]{1,0:T(8,128)(2,1)}, bf16[384,896]{1,0:T(8,128)(2,1)}, u32[]{:S(2)}, u32[]{:S(2)}) collective-permute-start(bf16[384,896]{1,0:T(8,128)(2,1)} %collective-permute-done.7.refs_9_.refs_10_), channel_id=1, source_target_pairs={{0,1},{1,0},{2,3},{3,2},{4,5},{5,4},{6,7},{7,6},{8,9},{9,8},{10,11... | collective-permute-start | bytes 2064392 | tf_op jit(solution)/shard_map/ppermute | solution.py:21
  69.2 2.3 %collective-permute-start.5 = (bf16[112,1280]{1,0:T(8,128)(2,1)}, bf16[112,1280]{1,0:T(8,128)(2,1)}, u32[]{:S(2)}, u32[]{:S(2)}) collective-permute-start(bf16[112,1280]{1,0:T(8,128)(2,1)} %copy-done.5), channel_id=1, source_target_pairs={{0,56},{8,0},{16,8},{24,16},{32,24},{40,32},{48,40},{56,48},{1,57}... | collective-permute-start | bytes 860168 | tf_op jit(solution)/shard_map/ppermute | solution.py:21
  73.7 2.6 %collective-permute-done.5.refs_6_ = bf16[112,1280]{1,0:T(8,128)(2,1)} collective-permute-done((bf16[112,1280]{1,0:T(8,128)(2,1)}, bf16[112,1280]{1,0:T(8,128)(2,1)}, u32[]{:S(2)}, u32[]{:S(2)}) %collective-permute-start.5) | collective-permute-done | bytes 286752 | tf_op jit(solution)/shard_map/ppermute | solution.py:21
  76.4 2.5 %collective-permute-done.6.refs_7_ = bf16[112,1280]{1,0:T(8,128)(2,1)} collective-permute-done((bf16[112,1280]{1,0:T(8,128)(2,1)}, bf16[112,1280]{1,0:T(8,128)(2,1)}, u32[]{:S(2)}, u32[]{:S(2)}) %collective-permute-start.6) | collective-permute-done | bytes 286752 | tf_op jit(solution)/shard_map/ppermute | solution.py:21
  82.1 13.1 %shard_map.37.refs_0_ = f32[2,8,1,384]{3,2,1,0:T(1,128)S(1)} custom-call(s32[20]{0:T(128)S(1)} %stack.129.place_ref, s32[384,128]{1,0:T(8,128)S(1)} %get-tuple-element.15.wanted_ref, bf16[112,1280]{1,0:T(8,128)(2,1)S(1)} %reshape.69.refs_0_, bf16[112,1280]{1,0:T(8,128)(2,1)S(1)} %copy-done.2, bf16[112,1280]{1,0:T(8,128)(2,1)S(1)} %copy-done.4, ...), custom_call_target="tpu_custom_call" | custom-call | flops 7046430720 | bytes 7798784 | tf_op jit(solution)/shard_map/pallas_call | solution.py:145
  95.2 13.5 %shard_map.38 = f32[2,8,1,384]{3,2,1,0:T(1,128)S(1)} custom-call(s32[20]{0:T(128)S(1)} %stack.127.place_ref, s32[384,128]{1,0:T(8,128)S(1)} %get-tuple-element.16.wanted_ref, f32[2,8,1,384]{3,2,1,0:T(1,128)S(1)} %shard_map.37.refs_0_, bf16[112,1152]{1,0:T(8,128)(2,1)S(1)} %reshape.71.refs_1_, bf16[112,1152]{1,0:T(8,128)(2,1)S(1)} %copy-done.8, ...), custom_call_target="tpu_custom_call" | custom-call | flops 6341787648 | bytes 7569408 | tf_op jit(solution)/shard_map/pallas_call | solution.py:145
  108.8 22.6 %all_to_all.15 = f32[32,2,8,256]{3,2,1,0:T(8,128)S(1)} all-to-all(f32[32,2,8,256]{3,2,1,0:T(8,128)S(1)} %bitcast.51), channel_id=1, replica_groups=mesh['x'=4,'z'=8,'y'=4,'c'=2] {'x','y','c'}, dimensions={0} | all-to-all | bytes 1048576 | tf_op jit(solution)/shard_map/all_to_all | solution.py:263
  132.2 5.6 %all-to-all-start.2 = ((f32[8,8,256]{2,1,0:T(8,128)}), f32[8,8,256]{2,1,0:T(8,128)S(1)}, u32[]{:S(2)}, u32[]{:S(2)}) async-start(f32[8,8,256]{2,1,0:T(8,128)} %broadcast_in_dim.5), calls=%async_computation.2 | async-start | bytes 131072 | tf_op jit(solution)/shard_map/all_to_all | solution.py:270
  137.8 7.4 %all-to-all-done.2 = f32[8,8,256]{2,1,0:T(8,128)S(1)} async-done(((f32[8,8,256]{2,1,0:T(8,128)}), f32[8,8,256]{2,1,0:T(8,128)S(1)}, u32[]{:S(2)}, u32[]{:S(2)}) %all-to-all-start.2) | async-done | bytes 65568 | tf_op jit(solution)/shard_map/all_to_all | solution.py:270
  (72 shorter events, 17.4 us)
Async XLA Ops:
  2.3 12.8 %all-to-all-start = ((bf16[4,28,2432]{2,1,0:T(8,128)(2,1)}), bf16[4,28,2432]{2,1,0:T(8,128)(2,1)}, u32[]{:S(2)}, u32[]{:S(2)}) async-start(bf16[4,28,2432]{2,1,0:T(8,128)(2,1)} %pad_maximum_fusion), calls=%async_computation | async-start | bytes 1245184 | tf_op jit(solution)/shard_map/all_to_all | solution.py:198
  15.0 14.9 %collective-permute-start.7 = (bf16[384,896]{1,0:T(8,128)(2,1)}, bf16[384,896]{1,0:T(8,128)(2,1)}, u32[]{:S(2)}, u32[]{:S(2)}) collective-permute-start(bf16[384,896]{1,0:T(8,128)(2,1)} %dynamic-slice_bitcast_fusion), channel_id=1, source_target_pairs={{0,64},{64,128},{128,192},{192,0},{1,65},{65,129},{129,193},{193,1... | collective-permute-start | bytes 2064392 | tf_op jit(solution)/shard_map/ppermute | solution.py:21
  16.4 22.1 %collective-permute-start.13 = (bf16[112,1152]{1,0:T(8,128)(2,1)S(1)}, bf16[112,1152]{1,0:T(8,128)(2,1)S(1)}, u32[]{:S(2)}, u32[]{:S(2)}) collective-permute-start(bf16[112,1152]{1,0:T(8,128)(2,1)S(1)} %reshape.71.refs_1_), channel_id=1, source_target_pairs={{0,8},{8,16},{16,24},{24,32},{32,40},{40,48},{48,56},{56,0},{1,9},... | collective-permute-start | bytes 774152 | tf_op jit(solution)/shard_map/ppermute | solution.py:21
  20.2 22.3 %collective-permute-start.14 = (bf16[112,1152]{1,0:T(8,128)(2,1)S(1)}, bf16[112,1152]{1,0:T(8,128)(2,1)}, u32[]{:S(2)}, u32[]{:S(2)}) collective-permute-start(bf16[112,1152]{1,0:T(8,128)(2,1)S(1)} %reshape.71.refs_1_), channel_id=1, source_target_pairs={{0,56},{8,0},{16,8},{24,16},{32,24},{40,32},{48,40},{56,48},{1,57}... | collective-permute-start | bytes 774152 | tf_op jit(solution)/shard_map/ppermute | solution.py:21
  24.2 44.4 %collective-permute-start.9 = (bf16[384,896]{1,0:T(8,128)(2,1)}, bf16[384,896]{1,0:T(8,128)(2,1)}, u32[]{:S(2)}, u32[]{:S(2)}) collective-permute-start(bf16[384,896]{1,0:T(8,128)(2,1)} %dynamic-slice_bitcast_fusion), channel_id=1, source_target_pairs={{0,192},{64,0},{128,64},{192,128},{1,193},{65,1},{129,65},{193,129... | collective-permute-start | bytes 2064392 | tf_op jit(solution)/shard_map/ppermute | solution.py:21
  29.9 38.7 %collective-permute-start.11 = (bf16[384,896]{1,0:T(8,128)(2,1)}, bf16[384,896]{1,0:T(8,128)(2,1)}, u32[]{:S(2)}, u32[]{:S(2)}) collective-permute-start(bf16[384,896]{1,0:T(8,128)(2,1)} %collective-permute-done.7.refs_9_.refs_10_), channel_id=1, source_target_pairs={{0,64},{64,128},{128,192},{192,0},{1,65},{65,129},{129,193},{193,1... | collective-permute-start | bytes 2064392 | tf_op jit(solution)/shard_map/ppermute | solution.py:21
  32.7 14.5 %collective-permute-start = (bf16[112,1280]{1,0:T(8,128)(2,1)S(1)}, bf16[112,1280]{1,0:T(8,128)(2,1)S(1)}, u32[]{:S(2)}, u32[]{:S(2)}) collective-permute-start(bf16[112,1280]{1,0:T(8,128)(2,1)S(1)} %reshape.69.refs_0_), channel_id=1, source_target_pairs={{0,8},{8,16},{16,24},{24,32},{32,40},{40,48},{48,56},{56,0},{1,9},... | collective-permute-start | bytes 860168 | tf_op jit(solution)/shard_map/ppermute | solution.py:21
  38.4 9.4 %collective-permute-start.1 = (bf16[112,1280]{1,0:T(8,128)(2,1)S(1)}, bf16[112,1280]{1,0:T(8,128)(2,1)S(1)}, u32[]{:S(2)}, u32[]{:S(2)}) collective-permute-start(bf16[112,1280]{1,0:T(8,128)(2,1)S(1)} %reshape.69.refs_0_), channel_id=1, source_target_pairs={{0,56},{8,0},{16,8},{24,16},{32,24},{40,32},{48,40},{56,48},{1,57}... | collective-permute-start | bytes 860168 | tf_op jit(solution)/shard_map/ppermute | solution.py:21
  42.5 10.2 %collective-permute-start.15 = (bf16[112,1152]{1,0:T(8,128)(2,1)S(1)}, bf16[112,1152]{1,0:T(8,128)(2,1)}, u32[]{:S(2)}, u32[]{:S(2)}) collective-permute-start(bf16[112,1152]{1,0:T(8,128)(2,1)S(1)} %collective-permute-done.13.refs_2_), channel_id=1, source_target_pairs={{0,8},{8,16},{16,24},{24,32},{32,40},{40,48},{48,56},{56,0},{1,9},... | collective-permute-start | bytes 774152 | tf_op jit(solution)/shard_map/ppermute | solution.py:21
  47.1 11.7 %collective-permute-start.2 = (bf16[112,1280]{1,0:T(8,128)(2,1)S(1)}, bf16[112,1280]{1,0:T(8,128)(2,1)}, u32[]{:S(2)}, u32[]{:S(2)}) collective-permute-start(bf16[112,1280]{1,0:T(8,128)(2,1)S(1)} %collective-permute-done.refs_1_), channel_id=1, source_target_pairs={{0,8},{8,16},{16,24},{24,32},{32,40},{40,48},{48,56},{56,0},{1,9},... | collective-permute-start | bytes 860168 | tf_op jit(solution)/shard_map/ppermute | solution.py:21
  47.9 11.0 %collective-permute-start.16 = (bf16[112,1152]{1,0:T(8,128)(2,1)}, bf16[112,1152]{1,0:T(8,128)(2,1)}, u32[]{:S(2)}, u32[]{:S(2)}) collective-permute-start(bf16[112,1152]{1,0:T(8,128)(2,1)} %collective-permute-done.14.refs_3_), channel_id=1, source_target_pairs={{0,56},{8,0},{16,8},{24,16},{32,24},{40,32},{48,40},{56,48},{1,57}... | collective-permute-start | bytes 774152 | tf_op jit(solution)/shard_map/ppermute | solution.py:21
  52.7 8.8 %collective-permute-start.3 = (bf16[112,1280]{1,0:T(8,128)(2,1)S(1)}, bf16[112,1280]{1,0:T(8,128)(2,1)S(1)}, u32[]{:S(2)}, u32[]{:S(2)}) collective-permute-start(bf16[112,1280]{1,0:T(8,128)(2,1)S(1)} %collective-permute-done.1.refs_2_), channel_id=1, source_target_pairs={{0,56},{8,0},{16,8},{24,16},{32,24},{40,32},{48,40},{56,48},{1,57}... | collective-permute-start | bytes 860168 | tf_op jit(solution)/shard_map/ppermute | solution.py:21
  58.8 12.6 %collective-permute-start.4 = (bf16[112,1280]{1,0:T(8,128)(2,1)}, bf16[112,1280]{1,0:T(8,128)(2,1)}, u32[]{:S(2)}, u32[]{:S(2)}) collective-permute-start(bf16[112,1280]{1,0:T(8,128)(2,1)} %collective-permute-done.2.refs_3_), channel_id=1, source_target_pairs={{0,8},{8,16},{16,24},{24,32},{32,40},{40,48},{48,56},{56,0},{1,9},... | collective-permute-start | bytes 860168 | tf_op jit(solution)/shard_map/ppermute | solution.py:21
  58.8 10.3 %collective-permute-start.18 = (bf16[112,1152]{1,0:T(8,128)(2,1)}, bf16[112,1152]{1,0:T(8,128)(2,1)S(1)}, u32[]{:S(2)}, u32[]{:S(2)}) collective-permute-start(bf16[112,1152]{1,0:T(8,128)(2,1)} %collective-permute-done.16.refs_5_), channel_id=1, source_target_pairs={{0,56},{8,0},{16,8},{24,16},{32,24},{40,32},{48,40},{56,48},{1,57}... | collective-permute-start | bytes 774152 | tf_op jit(solution)/shard_map/ppermute | solution.py:21
  62.2 16.9 %collective-permute-start.8 = (bf16[384,896]{1,0:T(8,128)(2,1)}, bf16[384,896]{1,0:T(8,128)(2,1)}, u32[]{:S(2)}, u32[]{:S(2)}) collective-permute-start(bf16[384,896]{1,0:T(8,128)(2,1)} %collective-permute-done.7.refs_9_.refs_10_), channel_id=1, source_target_pairs={{0,1},{1,0},{2,3},{3,2},{4,5},{5,4},{6,7},{7,6},{8,9},{9,8},{10,11... | collective-permute-start | bytes 2064392 | tf_op jit(solution)/shard_map/ppermute | solution.py:21
  68.6 10.5 %collective-permute-start.10 = (bf16[384,896]{1,0:T(8,128)(2,1)}, bf16[384,896]{1,0:T(8,128)(2,1)}, u32[]{:S(2)}, u32[]{:S(2)}) collective-permute-start(bf16[384,896]{1,0:T(8,128)(2,1)} %collective-permute-done.9.refs_11_.refs_12_), channel_id=1, source_target_pairs={{0,1},{1,0},{2,3},{3,2},{4,5},{5,4},{6,7},{7,6},{8,9},{9,8},{10,11... | collective-permute-start | bytes 2064392 | tf_op jit(solution)/shard_map/ppermute | solution.py:21
  68.7 10.5 %collective-permute-start.12 = (bf16[384,896]{1,0:T(8,128)(2,1)}, bf16[384,896]{1,0:T(8,128)(2,1)}, u32[]{:S(2)}, u32[]{:S(2)}) collective-permute-start(bf16[384,896]{1,0:T(8,128)(2,1)} %collective-permute-done.11.refs_13_.refs_14_), channel_id=1, source_target_pairs={{0,1},{1,0},{2,3},{3,2},{4,5},{5,4},{6,7},{7,6},{8,9},{9,8},{10,11... | collective-permute-start | bytes 2064392 | tf_op jit(solution)/shard_map/ppermute | solution.py:21
  69.2 7.2 %collective-permute-start.5 = (bf16[112,1280]{1,0:T(8,128)(2,1)}, bf16[112,1280]{1,0:T(8,128)(2,1)}, u32[]{:S(2)}, u32[]{:S(2)}) collective-permute-start(bf16[112,1280]{1,0:T(8,128)(2,1)} %copy-done.5), channel_id=1, source_target_pairs={{0,56},{8,0},{16,8},{24,16},{32,24},{40,32},{48,40},{56,48},{1,57}... | collective-permute-start | bytes 860168 | tf_op jit(solution)/shard_map/ppermute | solution.py:21
  71.4 7.4 %collective-permute-start.6 = (bf16[112,1280]{1,0:T(8,128)(2,1)}, bf16[112,1280]{1,0:T(8,128)(2,1)}, u32[]{:S(2)}, u32[]{:S(2)}) collective-permute-start(bf16[112,1280]{1,0:T(8,128)(2,1)} %collective-permute-done.4.refs_5_), channel_id=1, source_target_pairs={{0,8},{8,16},{16,24},{24,32},{32,40},{40,48},{48,56},{56,0},{1,9},... | collective-permute-start | bytes 860168 | tf_op jit(solution)/shard_map/ppermute | solution.py:21
  76.3 18.8 %collective-permute-start.17 = (bf16[112,1152]{1,0:T(8,128)(2,1)}, bf16[112,1152]{1,0:T(8,128)(2,1)S(1)}, u32[]{:S(2)}, u32[]{:S(2)}) collective-permute-start(bf16[112,1152]{1,0:T(8,128)(2,1)} %collective-permute-done.15.refs_4_), channel_id=1, source_target_pairs={{0,8},{8,16},{16,24},{24,32},{32,40},{40,48},{48,56},{56,0},{1,9},... | collective-permute-start | bytes 774152 | tf_op jit(solution)/shard_map/ppermute | solution.py:21
  78.9 16.3 %collective-permute-start.19 = (bf16[112,1152]{1,0:T(8,128)(2,1)}, bf16[112,1152]{1,0:T(8,128)(2,1)S(1)}, u32[]{:S(2)}, u32[]{:S(2)}) collective-permute-start(bf16[112,1152]{1,0:T(8,128)(2,1)} %copy-done.9), channel_id=1, source_target_pairs={{0,56},{8,0},{16,8},{24,16},{32,24},{40,32},{48,40},{56,48},{1,57}... | collective-permute-start | bytes 774152 | tf_op jit(solution)/shard_map/ppermute | solution.py:21
  82.0 13.1 %copy-start.8 = (bf16[112,1152]{1,0:T(8,128)(2,1)S(1)}, bf16[112,1152]{1,0:T(8,128)(2,1)}, u32[]{:S(2)}) copy-start(bf16[112,1152]{1,0:T(8,128)(2,1)} %copy-done.7) | copy-start | bytes 774148
  82.0 13.2 %copy-start.10 = (bf16[112,1152]{1,0:T(8,128)(2,1)S(1)}, bf16[112,1152]{1,0:T(8,128)(2,1)}, u32[]{:S(2)}) copy-start(bf16[112,1152]{1,0:T(8,128)(2,1)} %copy-done.9) | copy-start | bytes 774148
  132.2 13.0 %all-to-all-start.2 = ((f32[8,8,256]{2,1,0:T(8,128)}), f32[8,8,256]{2,1,0:T(8,128)S(1)}, u32[]{:S(2)}, u32[]{:S(2)}) async-start(f32[8,8,256]{2,1,0:T(8,128)} %broadcast_in_dim.5), calls=%async_computation.2 | async-start | bytes 131072 | tf_op jit(solution)/shard_map/all_to_all | solution.py:270
  (9 other events, 16.4 us)
where the time goes:
time: 147 us; the launch traced here: 146 us
  starting transfers between devices  46.7 us (32%)
  waiting for transfers between devices  31.4 us (21%)
  Pallas kernels  26.6 us (18%)
  blocking collectives  22.6 us (15%)
  local copies, waits for them, and re-layouts  12.6 us (9%)
  other arithmetic  3.32 us (2%)
  matrix products  2.66 us (2%)
    ppermute x20, starting transfers between devices, shift(): return lax.ppermute(x, axis, [(i, (i + by) % size) for i in range(size)])  36.3 us
    pallas_call x2, Pallas kernels, local_stats(): pl.pallas_call(functools.partial(loss_kernel, sizes=sizes, counts=counts,...  26.6 us
    all_to_all x1, blocking collectives, body(): got = lax.all_to_all(sent, ('x', 'y', 'c'), 0, 0, tiled=True)  22.6 us
    ppermute x20, waiting for transfers between devices, shift(): return lax.ppermute(x, axis, [(i, (i + by) % size) for i in range(size)])  18.9 us
    all_to_all x1, waiting for transfers between devices, body(): lax.all_to_all(jnp.broadcast_to(losses[None], (nz, *losses.shape)), 'z',...  7.39 us
    unnamed x23, local copies, waits for them, and re-layouts  5.72 us
    all_to_all x1, starting transfers between devices, body(): lax.all_to_all(jnp.broadcast_to(losses[None], (nz, *losses.shape)), 'z',...  5.59 us
    all_to_all x1, waiting for transfers between devices, body(): own = lax.all_to_all(blocks, 'x', 0, 0, tiled=True)  5.18 us
  transfers between devices with their start and end apart: 22, of which 8 were waited for; matrix products, arithmetic and copies ran while one was open for 6% of the time, Pallas kernels for 9%

commit v1 on v0

--- a/solution.py
+++ b/solution.py
@@ -83,22 +83,24 @@
     def finish(block):
         for r in range(0, rows_each, LANES):
             some = slice(r, r + LANES)
-            tops = jnp.transpose(top[some, :])
-            totals = jnp.transpose(total[some, :])
-            chosen = jnp.transpose(picked[some, :])
-            high = jnp.max(tops, axis=0, keepdims=True)
-            summed = jnp.sum(totals * jnp.exp(tops - high), axis=0, keepdims=True)
-            chosen = jnp.sum(chosen, axis=0, keepdims=True)
+            lane = lax.broadcasted_iota(jnp.int32, (LANES, LANES), 1)
+            high = jnp.max(top[some, :], axis=1, keepdims=True)
+            summed = total[some, :] * jnp.exp(top[some, :] - high)
+            summed = jnp.sum(summed, axis=1, keepdims=True)
+            chosen = jnp.sum(picked[some, :], axis=1, keepdims=True)
+            both = jnp.transpose(jnp.where(lane == 0, high + jnp.log(summed), chosen))
+            high, chosen = both[0:1, :], both[1:2, :]
             row = place_ref[pieces + 1 + block] + r // tokens
             at = slice(r % tokens, r % tokens + LANES)
             if merged:
-                before = earlier_ref[0, row, :, at]
+                before = earlier_ref[row, :, at]
                 joined = jnp.maximum(before, high)
-                summed = summed * jnp.exp(high - joined) + jnp.exp(before - joined)
-                high = joined
-                chosen = chosen + earlier_ref[1, row, :, at]
-            out_ref[0, row, :, at] = high + jnp.log(summed)
-            out_ref[1, row, :, at] = chosen
+                high = joined + jnp.log(
+                    jnp.exp(high - joined) + jnp.exp(before - joined)
+                )
+                chosen = chosen + earlier_ref[row + 4, :, at]
+            out_ref[row, :, at] = high
+            out_ref[row + 4, :, at] = chosen
 
     starts = [sum(tiles[:k]) for k in range(len(tiles))]
     last = (2, starts[-1], tiles[-1])
@@ -147,7 +149,7 @@
             loss_kernel, sizes=sizes, counts=counts, masked=masked, merged=len(earlier)
         ),
         out_shape=jax.ShapeDtypeStruct(
-            (2, blocks * rows_each // wanted.shape[0], 1, wanted.shape[0]), jnp.float32
+            (2 * blocks * rows_each // wanted.shape[0], 1, wanted.shape[0]), jnp.float32
         ),
         in_specs=[
             pl.BlockSpec(memory_space=pltpu.SMEM),
@@ -230,7 +232,8 @@
     row_blocks = [[(ordered, 0)]]
     for rows in (left, right, shift(left, "x", 1)):
         row_blocks.append([(rows, c * tokens), (shift(rows, "c", 1), (1 - c) * tokens)])
-    spots = [(x + k) % nx * draws for k in (0, nx - 1, 1, 2)]
+    spots = [(x + k) % nx for k in (0, nx - 1, 1, 2)]
+    spots = [at // nc * (4 * draws) + at % nc * draws for at in spots]
 
     first_column = (y * nc + c) * columns + x * WIDTH
     wanted = (
@@ -248,7 +251,7 @@
         limit - WIDTHS[0],
         256,
         (first,),
-    )[:, :, 0]
+    ).reshape(nc, 4 * draws, tokens)
 
     sent = jnp.stack(
         [
@@ -257,18 +260,23 @@
         ]
     )
     sent = jnp.broadcast_to(
-        sent[:, None], (len(sent), nx // len(sent) * ny * nc, *sent.shape[1:])
-    )
-    sent = sent.reshape(nx * ny * nc, *sent.shape[2:])
+        sent[:, None], (len(sent), nx // len(sent) * ny, *sent.shape[1:])
+    )
+    sent = sent.reshape(nx * ny * nc, *sent.shape[3:])
     got = lax.all_to_all(sent, ("x", "y", "c"), 0, 0, tiled=True)
-    high = jnp.max(got[:, 0], axis=0)
+    logs, chosen = got[:, : 2 * draws], got[:, 2 * draws :]
+    high = jnp.max(logs, axis=0)
     losses = (
         high
-        + jnp.log(jnp.sum(jnp.exp(got[:, 0] - high[None]), axis=0))
-        - jnp.sum(got[:, 1], axis=0)
+        + jnp.log(jnp.sum(jnp.exp(logs - high[None]), axis=0))
+        - jnp.sum(chosen, axis=0)
     )
     got = lax.all_to_all(
-        jnp.broadcast_to(losses[None], (nz, *losses.shape)), "z", 0, 0, tiled=True
+        jnp.broadcast_to(losses[None], (nz * nc, *losses.shape)),
+        ("z", "c"),
+        0,
+        0,
+        tiled=True,
     )
     got = got.reshape(-1, got.shape[-1])
     each = TRAIN // (nx * nz)

time: 147 us -> 145 us (0.986)
  blocking collectives: 22.6 us -> 20 us
    all_to_all x1, blocking collectives: 22.6 us -> 20 us  [body(): got = lax.all_to_all(sent, ('x', 'y', 'c'), 0, 0, tiled=True)]
where the time goes in v1:
time: 145 us; the launch traced here: 144 us
  starting transfers between devices  47.2 us (33%)
  waiting for transfers between devices  31.8 us (22%)
  Pallas kernels  26.3 us (18%)
  blocking collectives  20 us (14%)
  local copies, waits for them, and re-layouts  12.6 us (9%)
  other arithmetic  3.36 us (2%)
  matrix products  2.66 us (2%)
    ppermute x20, starting transfers between devices, shift(): return lax.ppermute(x, axis, [(i, (i + by) % size) for i in range(size)])  36.3 us
    pallas_call x2, Pallas kernels, local_stats(): pl.pallas_call(functools.partial(loss_kernel, sizes=sizes, counts=counts,...  26.3 us
    all_to_all x1, blocking collectives, body(): got = lax.all_to_all(sent, ('x', 'y', 'c'), 0, 0, tiled=True)  20 us
    ppermute x20, waiting for transfers between devices, shift(): return lax.ppermute(x, axis, [(i, (i + by) % size) for i in range(size)])  18.9 us
    all_to_all x1, waiting for transfers between devices, body(): lax.all_to_all(jnp.broadcast_to(losses[None], (nz * nc, *losses.shape)),...  7.77 us
    all_to_all x1, starting transfers between devices, body(): lax.all_to_all(jnp.broadcast_to(losses[None], (nz * nc, *losses.shape)),...  6.08 us
    unnamed x23, local copies, waits for them, and re-layouts  5.72 us
    all_to_all x1, waiting for transfers between devices, body(): own = lax.all_to_all(blocks, 'x', 0, 0, tiled=True)  5.18 us
  transfers between devices with their start and end apart: 22, of which 8 were waited for; matrix products, arithmetic and copies ran while one was open for 6% of the time, Pallas kernels for 9%

profile of v1, /device:TPU:1, one launch (start us, length us, event | category | flops | bytes accessed | tf_op | source)
XLA Modules:
  0.0 144.2 jit_solution(14621064115066969156)
XLA Ops:
  2.3 4.8 %all-to-all-start = ((bf16[4,28,2432]{2,1,0:T(8,128)(2,1)}), bf16[4,28,2432]{2,1,0:T(8,128)(2,1)}, u32[]{:S(2)}, u32[]{:S(2)}) async-start(bf16[4,28,2432]{2,1,0:T(8,128)(2,1)} %pad_maximum_fusion), calls=%async_computation | async-start | bytes 1245184 | tf_op jit(solution)/shard_map/all_to_all | solution.py:200
  7.1 1.8 %fusion.1 = bf16[896,768]{0,1:T(8,128)(2,1)S(1)} fusion(bf16[768,896]{1,0:T(8,128)(2,1)S(1)} %bitcast.41, s32[896]{0:T(1024)S(1)} %fusion.18), kind=kOutput, calls=%fused_computation.2 | convolution fusion | flops 1234616320 | bytes 2756096 | tf_op jit(solution)/shard_map/dot_general | solution.py:224
  9.9 5.2 %all-to-all-done = bf16[4,28,2432]{2,1,0:T(8,128)(2,1)} async-done(((bf16[4,28,2432]{2,1,0:T(8,128)(2,1)}), bf16[4,28,2432]{2,1,0:T(8,128)(2,1)}, u32[]{:S(2)}, u32[]{:S(2)}) %all-to-all-start) | async-done | bytes 544800 | tf_op jit(solution)/shard_map/all_to_all | solution.py:200
  16.4 3.8 %collective-permute-start.13 = (bf16[112,1152]{1,0:T(8,128)(2,1)S(1)}, bf16[112,1152]{1,0:T(8,128)(2,1)S(1)}, u32[]{:S(2)}, u32[]{:S(2)}) collective-permute-start(bf16[112,1152]{1,0:T(8,128)(2,1)S(1)} %reshape.74.refs_1_), channel_id=1, source_target_pairs={{0,8},{8,16},{16,24},{24,32},{32,40},{40,48},{48,56},{56,0},{1,9},... | collective-permute-start | bytes 774152 | tf_op jit(solution)/shard_map/ppermute | solution.py:21
  20.2 4.0 %collective-permute-start.14 = (bf16[112,1152]{1,0:T(8,128)(2,1)S(1)}, bf16[112,1152]{1,0:T(8,128)(2,1)}, u32[]{:S(2)}, u32[]{:S(2)}) collective-permute-start(bf16[112,1152]{1,0:T(8,128)(2,1)S(1)} %reshape.74.refs_1_), channel_id=1, source_target_pairs={{0,56},{8,0},{16,8},{24,16},{32,24},{40,32},{48,40},{56,48},{1,57}... | collective-permute-start | bytes 774152 | tf_op jit(solution)/shard_map/ppermute | solution.py:21
  24.2 2.4 %collective-permute-start.9 = (bf16[384,896]{1,0:T(8,128)(2,1)}, bf16[384,896]{1,0:T(8,128)(2,1)}, u32[]{:S(2)}, u32[]{:S(2)}) collective-permute-start(bf16[384,896]{1,0:T(8,128)(2,1)} %dynamic-slice_bitcast_fusion), channel_id=1, source_target_pairs={{0,192},{64,0},{128,64},{192,128},{1,193},{65,1},{129,65},{193,129... | collective-permute-start | bytes 2064392 | tf_op jit(solution)/shard_map/ppermute | solution.py:21
  26.6 3.3 %collective-permute-done.7.refs_9_.refs_10_ = bf16[384,896]{1,0:T(8,128)(2,1)} collective-permute-done((bf16[384,896]{1,0:T(8,128)(2,1)}, bf16[384,896]{1,0:T(8,128)(2,1)}, u32[]{:S(2)}, u32[]{:S(2)}) %collective-permute-start.7) | collective-permute-done | bytes 688160 | tf_op jit(solution)/shard_map/ppermute | solution.py:21
  29.9 1.7 %slice.50 = bf16[4,28,1280]{2,1,0:T(8,128)(2,1)} slice(bf16[4,28,2432]{2,1,0:T(8,128)(2,1)} %all-to-all-done), slice={[0:4], [0:28], [0:1280]} | slice | bytes 573440 | tf_op jit(solution)/shard_map/slice | solution.py:204
  32.7 5.7 %collective-permute-start = (bf16[112,1280]{1,0:T(8,128)(2,1)S(1)}, bf16[112,1280]{1,0:T(8,128)(2,1)S(1)}, u32[]{:S(2)}, u32[]{:S(2)}) collective-permute-start(bf16[112,1280]{1,0:T(8,128)(2,1)S(1)} %reshape.72.refs_0_), channel_id=1, source_target_pairs={{0,8},{8,16},{16,24},{24,32},{32,40},{40,48},{48,56},{56,0},{1,9},... | collective-permute-start | bytes 860168 | tf_op jit(solution)/shard_map/ppermute | solution.py:21
  38.4 4.0 %collective-permute-start.1 = (bf16[112,1280]{1,0:T(8,128)(2,1)S(1)}, bf16[112,1280]{1,0:T(8,128)(2,1)S(1)}, u32[]{:S(2)}, u32[]{:S(2)}) collective-permute-start(bf16[112,1280]{1,0:T(8,128)(2,1)S(1)} %reshape.72.refs_0_), channel_id=1, source_target_pairs={{0,56},{8,0},{16,8},{24,16},{32,24},{40,32},{48,40},{56,48},{1,57}... | collective-permute-start | bytes 860168 | tf_op jit(solution)/shard_map/ppermute | solution.py:21
  43.2 4.0 %collective-permute-done.refs_1_ = bf16[112,1280]{1,0:T(8,128)(2,1)S(1)} collective-permute-done((bf16[112,1280]{1,0:T(8,128)(2,1)S(1)}, bf16[112,1280]{1,0:T(8,128)(2,1)S(1)}, u32[]{:S(2)}, u32[]{:S(2)}) %collective-permute-start) | collective-permute-done | bytes 286752 | tf_op jit(solution)/shard_map/ppermute | solution.py:21
  47.9 2.7 %collective-permute-start.16 = (bf16[112,1152]{1,0:T(8,128)(2,1)}, bf16[112,1152]{1,0:T(8,128)(2,1)}, u32[]{:S(2)}, u32[]{:S(2)}) collective-permute-start(bf16[112,1152]{1,0:T(8,128)(2,1)} %collective-permute-done.14.refs_3_), channel_id=1, source_target_pairs={{0,56},{8,0},{16,8},{24,16},{32,24},{40,32},{48,40},{56,48},{1,57}... | collective-permute-start | bytes 774152 | tf_op jit(solution)/shard_map/ppermute | solution.py:21
  50.5 2.1 %collective-permute-done.15.refs_4_ = bf16[112,1152]{1,0:T(8,128)(2,1)} collective-permute-done((bf16[112,1152]{1,0:T(8,128)(2,1)S(1)}, bf16[112,1152]{1,0:T(8,128)(2,1)}, u32[]{:S(2)}, u32[]{:S(2)}) %collective-permute-start.15) | collective-permute-done | bytes 258080 | tf_op jit(solution)/shard_map/ppermute | solution.py:21
  54.6 4.2 %collective-permute-done.2.refs_3_ = bf16[112,1280]{1,0:T(8,128)(2,1)} collective-permute-done((bf16[112,1280]{1,0:T(8,128)(2,1)S(1)}, bf16[112,1280]{1,0:T(8,128)(2,1)}, u32[]{:S(2)}, u32[]{:S(2)}) %collective-permute-start.2) | collective-permute-done | bytes 286752 | tf_op jit(solution)/shard_map/ppermute | solution.py:21
  58.8 2.7 %collective-permute-start.18 = (bf16[112,1152]{1,0:T(8,128)(2,1)}, bf16[112,1152]{1,0:T(8,128)(2,1)S(1)}, u32[]{:S(2)}, u32[]{:S(2)}) collective-permute-start(bf16[112,1152]{1,0:T(8,128)(2,1)} %collective-permute-done.16.refs_5_), channel_id=1, source_target_pairs={{0,56},{8,0},{16,8},{24,16},{32,24},{40,32},{48,40},{56,48},{1,57}... | collective-permute-start | bytes 774152 | tf_op jit(solution)/shard_map/ppermute | solution.py:21
  62.2 6.4 %collective-permute-start.8 = (bf16[384,896]{1,0:T(8,128)(2,1)}, bf16[384,896]{1,0:T(8,128)(2,1)}, u32[]{:S(2)}, u32[]{:S(2)}) collective-permute-start(bf16[384,896]{1,0:T(8,128)(2,1)} %collective-permute-done.7.refs_9_.refs_10_), channel_id=1, source_target_pairs={{0,1},{1,0},{2,3},{3,2},{4,5},{5,4},{6,7},{7,6},{8,9},{9,8},{10,11... | collective-permute-start | bytes 2064392 | tf_op jit(solution)/shard_map/ppermute | solution.py:21
  69.2 2.3 %collective-permute-start.5 = (bf16[112,1280]{1,0:T(8,128)(2,1)}, bf16[112,1280]{1,0:T(8,128)(2,1)}, u32[]{:S(2)}, u32[]{:S(2)}) collective-permute-start(bf16[112,1280]{1,0:T(8,128)(2,1)} %copy-done.5), channel_id=1, source_target_pairs={{0,56},{8,0},{16,8},{24,16},{32,24},{40,32},{48,40},{56,48},{1,57}... | collective-permute-start | bytes 860168 | tf_op jit(solution)/shard_map/ppermute | solution.py:21
  73.7 2.6 %collective-permute-done.5.refs_6_ = bf16[112,1280]{1,0:T(8,128)(2,1)} collective-permute-done((bf16[112,1280]{1,0:T(8,128)(2,1)}, bf16[112,1280]{1,0:T(8,128)(2,1)}, u32[]{:S(2)}, u32[]{:S(2)}) %collective-permute-start.5) | collective-permute-done | bytes 286752 | tf_op jit(solution)/shard_map/ppermute | solution.py:21
  76.4 2.5 %collective-permute-done.6.refs_7_ = bf16[112,1280]{1,0:T(8,128)(2,1)} collective-permute-done((bf16[112,1280]{1,0:T(8,128)(2,1)}, bf16[112,1280]{1,0:T(8,128)(2,1)}, u32[]{:S(2)}, u32[]{:S(2)}) %collective-permute-start.6) | collective-permute-done | bytes 286752 | tf_op jit(solution)/shard_map/ppermute | solution.py:21
  82.1 13.1 %shard_map.37.refs_0_ = f32[16,1,384]{2,1,0:T(1,128)S(1)} custom-call(s32[20]{0:T(128)S(1)} %stack.129.place_ref, s32[384,128]{1,0:T(8,128)S(1)} %get-tuple-element.15.wanted_ref, bf16[112,1280]{1,0:T(8,128)(2,1)S(1)} %reshape.72.refs_0_, bf16[112,1280]{1,0:T(8,128)(2,1)S(1)} %copy-done.2, bf16[112,1280]{1,0:T(8,128)(2,1)S(1)} %copy-done.4, ...), custom_call_target="tpu_custom_call" | custom-call | flops 7046430720 | bytes 7798784 | tf_op jit(solution)/shard_map/pallas_call | solution.py:147
  95.2 13.2 %shard_map.38 = f32[16,1,384]{2,1,0:T(1,128)S(1)} custom-call(s32[20]{0:T(128)S(1)} %stack.127.place_ref, s32[384,128]{1,0:T(8,128)S(1)} %get-tuple-element.16.wanted_ref, f32[16,1,384]{2,1,0:T(1,128)S(1)} %shard_map.37.refs_0_, bf16[112,1152]{1,0:T(8,128)(2,1)S(1)} %reshape.74.refs_1_, bf16[112,1152]{1,0:T(8,128)(2,1)S(1)} %copy-done.8, ...), custom_call_target="tpu_custom_call" | custom-call | flops 6341787648 | bytes 7569408 | tf_op jit(solution)/shard_map/pallas_call | solution.py:147
  108.5 20.0 %all_to_all.15 = f32[32,8,256]{2,1,0:T(8,128)S(1)} all-to-all(f32[32,8,256]{2,1,0:T(8,128)S(1)} %bitcast.44), channel_id=1, replica_groups=mesh['x'=4,'z'=8,'y'=4,'c'=2] {'x','y','c'}, dimensions={0} | all-to-all | bytes 524288 | tf_op jit(solution)/shard_map/all_to_all | solution.py:266
  129.3 6.1 %all-to-all-start.2 = ((f32[16,4,256]{2,1,0:T(4,128)}), f32[16,4,256]{2,1,0:T(4,128)S(1)}, u32[]{:S(2)}, u32[]{:S(2)}) async-start(f32[16,4,256]{2,1,0:T(4,128)} %broadcast_in_dim.5), calls=%async_computation.2 | async-start | bytes 131072 | tf_op jit(solution)/shard_map/all_to_all | solution.py:274
  135.4 7.8 %all-to-all-done.2 = f32[16,4,256]{2,1,0:T(4,128)S(1)} async-done(((f32[16,4,256]{2,1,0:T(4,128)}), f32[16,4,256]{2,1,0:T(4,128)S(1)}, u32[]{:S(2)}, u32[]{:S(2)}) %all-to-all-start.2) | async-done | bytes 65568 | tf_op jit(solution)/shard_map/all_to_all | solution.py:274
  (73 shorter events, 17.4 us)
Async XLA Ops:
  2.3 12.8 %all-to-all-start = ((bf16[4,28,2432]{2,1,0:T(8,128)(2,1)}), bf16[4,28,2432]{2,1,0:T(8,128)(2,1)}, u32[]{:S(2)}, u32[]{:S(2)}) async-start(bf16[4,28,2432]{2,1,0:T(8,128)(2,1)} %pad_maximum_fusion), calls=%async_computation | async-start | bytes 1245184 | tf_op jit(solution)/shard_map/all_to_all | solution.py:200
  15.0 14.9 %collective-permute-start.7 = (bf16[384,896]{1,0:T(8,128)(2,1)}, bf16[384,896]{1,0:T(8,128)(2,1)}, u32[]{:S(2)}, u32[]{:S(2)}) collective-permute-start(bf16[384,896]{1,0:T(8,128)(2,1)} %dynamic-slice_bitcast_fusion), channel_id=1, source_target_pairs={{0,64},{64,128},{128,192},{192,0},{1,65},{65,129},{129,193},{193,1... | collective-permute-start | bytes 2064392 | tf_op jit(solution)/shard_map/ppermute | solution.py:21
  16.4 22.1 %collective-permute-start.13 = (bf16[112,1152]{1,0:T(8,128)(2,1)S(1)}, bf16[112,1152]{1,0:T(8,128)(2,1)S(1)}, u32[]{:S(2)}, u32[]{:S(2)}) collective-permute-start(bf16[112,1152]{1,0:T(8,128)(2,1)S(1)} %reshape.74.refs_1_), channel_id=1, source_target_pairs={{0,8},{8,16},{16,24},{24,32},{32,40},{40,48},{48,56},{56,0},{1,9},... | collective-permute-start | bytes 774152 | tf_op jit(solution)/shard_map/ppermute | solution.py:21
  20.2 22.3 %collective-permute-start.14 = (bf16[112,1152]{1,0:T(8,128)(2,1)S(1)}, bf16[112,1152]{1,0:T(8,128)(2,1)}, u32[]{:S(2)}, u32[]{:S(2)}) collective-permute-start(bf16[112,1152]{1,0:T(8,128)(2,1)S(1)} %reshape.74.refs_1_), channel_id=1, source_target_pairs={{0,56},{8,0},{16,8},{24,16},{32,24},{40,32},{48,40},{56,48},{1,57}... | collective-permute-start | bytes 774152 | tf_op jit(solution)/shard_map/ppermute | solution.py:21
  24.2 44.4 %collective-permute-start.9 = (bf16[384,896]{1,0:T(8,128)(2,1)}, bf16[384,896]{1,0:T(8,128)(2,1)}, u32[]{:S(2)}, u32[]{:S(2)}) collective-permute-start(bf16[384,896]{1,0:T(8,128)(2,1)} %dynamic-slice_bitcast_fusion), channel_id=1, source_target_pairs={{0,192},{64,0},{128,64},{192,128},{1,193},{65,1},{129,65},{193,129... | collective-permute-start | bytes 2064392 | tf_op jit(solution)/shard_map/ppermute | solution.py:21
  29.9 38.7 %collective-permute-start.11 = (bf16[384,896]{1,0:T(8,128)(2,1)}, bf16[384,896]{1,0:T(8,128)(2,1)}, u32[]{:S(2)}, u32[]{:S(2)}) collective-permute-start(bf16[384,896]{1,0:T(8,128)(2,1)} %collective-permute-done.7.refs_9_.refs_10_), channel_id=1, source_target_pairs={{0,64},{64,128},{128,192},{192,0},{1,65},{65,129},{129,193},{193,1... | collective-permute-start | bytes 2064392 | tf_op jit(solution)/shard_map/ppermute | solution.py:21
  32.7 14.5 %collective-permute-start = (bf16[112,1280]{1,0:T(8,128)(2,1)S(1)}, bf16[112,1280]{1,0:T(8,128)(2,1)S(1)}, u32[]{:S(2)}, u32[]{:S(2)}) collective-permute-start(bf16[112,1280]{1,0:T(8,128)(2,1)S(1)} %reshape.72.refs_0_), channel_id=1, source_target_pairs={{0,8},{8,16},{16,24},{24,32},{32,40},{40,48},{48,56},{56,0},{1,9},... | collective-permute-start | bytes 860168 | tf_op jit(solution)/shard_map/ppermute | solution.py:21
  38.4 9.4 %collective-permute-start.1 = (bf16[112,1280]{1,0:T(8,128)(2,1)S(1)}, bf16[112,1280]{1,0:T(8,128)(2,1)S(1)}, u32[]{:S(2)}, u32[]{:S(2)}) collective-permute-start(bf16[112,1280]{1,0:T(8,128)(2,1)S(1)} %reshape.72.refs_0_), channel_id=1, source_target_pairs={{0,56},{8,0},{16,8},{24,16},{32,24},{40,32},{48,40},{56,48},{1,57}... | collective-permute-start | bytes 860168 | tf_op jit(solution)/shard_map/ppermute | solution.py:21
  42.5 10.2 %collective-permute-start.15 = (bf16[112,1152]{1,0:T(8,128)(2,1)S(1)}, bf16[112,1152]{1,0:T(8,128)(2,1)}, u32[]{:S(2)}, u32[]{:S(2)}) collective-permute-start(bf16[112,1152]{1,0:T(8,128)(2,1)S(1)} %collective-permute-done.13.refs_2_), channel_id=1, source_target_pairs={{0,8},{8,16},{16,24},{24,32},{32,40},{40,48},{48,56},{56,0},{1,9},... | collective-permute-start | bytes 774152 | tf_op jit(solution)/shard_map/ppermute | solution.py:21
  47.1 11.7 %collective-permute-start.2 = (bf16[112,1280]{1,0:T(8,128)(2,1)S(1)}, bf16[112,1280]{1,0:T(8,128)(2,1)}, u32[]{:S(2)}, u32[]{:S(2)}) collective-permute-start(bf16[112,1280]{1,0:T(8,128)(2,1)S(1)} %collective-permute-done.refs_1_), channel_id=1, source_target_pairs={{0,8},{8,16},{16,24},{24,32},{32,40},{40,48},{48,56},{56,0},{1,9},... | collective-permute-start | bytes 860168 | tf_op jit(solution)/shard_map/ppermute | solution.py:21
  47.9 11.0 %collective-permute-start.16 = (bf16[112,1152]{1,0:T(8,128)(2,1)}, bf16[112,1152]{1,0:T(8,128)(2,1)}, u32[]{:S(2)}, u32[]{:S(2)}) collective-permute-start(bf16[112,1152]{1,0:T(8,128)(2,1)} %collective-permute-done.14.refs_3_), channel_id=1, source_target_pairs={{0,56},{8,0},{16,8},{24,16},{32,24},{40,32},{48,40},{56,48},{1,57}... | collective-permute-start | bytes 774152 | tf_op jit(solution)/shard_map/ppermute | solution.py:21
  52.7 8.8 %collective-permute-start.3 = (bf16[112,1280]{1,0:T(8,128)(2,1)S(1)}, bf16[112,1280]{1,0:T(8,128)(2,1)S(1)}, u32[]{:S(2)}, u32[]{:S(2)}) collective-permute-start(bf16[112,1280]{1,0:T(8,128)(2,1)S(1)} %collective-permute-done.1.refs_2_), channel_id=1, source_target_pairs={{0,56},{8,0},{16,8},{24,16},{32,24},{40,32},{48,40},{56,48},{1,57}... | collective-permute-start | bytes 860168 | tf_op jit(solution)/shard_map/ppermute | solution.py:21
  58.8 12.6 %collective-permute-start.4 = (bf16[112,1280]{1,0:T(8,128)(2,1)}, bf16[112,1280]{1,0:T(8,128)(2,1)}, u32[]{:S(2)}, u32[]{:S(2)}) collective-permute-start(bf16[112,1280]{1,0:T(8,128)(2,1)} %collective-permute-done.2.refs_3_), channel_id=1, source_target_pairs={{0,8},{8,16},{16,24},{24,32},{32,40},{40,48},{48,56},{56,0},{1,9},... | collective-permute-start | bytes 860168 | tf_op jit(solution)/shard_map/ppermute | solution.py:21
  58.8 10.3 %collective-permute-start.18 = (bf16[112,1152]{1,0:T(8,128)(2,1)}, bf16[112,1152]{1,0:T(8,128)(2,1)S(1)}, u32[]{:S(2)}, u32[]{:S(2)}) collective-permute-start(bf16[112,1152]{1,0:T(8,128)(2,1)} %collective-permute-done.16.refs_5_), channel_id=1, source_target_pairs={{0,56},{8,0},{16,8},{24,16},{32,24},{40,32},{48,40},{56,48},{1,57}... | collective-permute-start | bytes 774152 | tf_op jit(solution)/shard_map/ppermute | solution.py:21
  62.2 16.9 %collective-permute-start.8 = (bf16[384,896]{1,0:T(8,128)(2,1)}, bf16[384,896]{1,0:T(8,128)(2,1)}, u32[]{:S(2)}, u32[]{:S(2)}) collective-permute-start(bf16[384,896]{1,0:T(8,128)(2,1)} %collective-permute-done.7.refs_9_.refs_10_), channel_id=1, source_target_pairs={{0,1},{1,0},{2,3},{3,2},{4,5},{5,4},{6,7},{7,6},{8,9},{9,8},{10,11... | collective-permute-start | bytes 2064392 | tf_op jit(solution)/shard_map/ppermute | solution.py:21
  68.6 10.5 %collective-permute-start.10 = (bf16[384,896]{1,0:T(8,128)(2,1)}, bf16[384,896]{1,0:T(8,128)(2,1)}, u32[]{:S(2)}, u32[]{:S(2)}) collective-permute-start(bf16[384,896]{1,0:T(8,128)(2,1)} %collective-permute-done.9.refs_11_.refs_12_), channel_id=1, source_target_pairs={{0,1},{1,0},{2,3},{3,2},{4,5},{5,4},{6,7},{7,6},{8,9},{9,8},{10,11... | collective-permute-start | bytes 2064392 | tf_op jit(solution)/shard_map/ppermute | solution.py:21
  68.7 10.5 %collective-permute-start.12 = (bf16[384,896]{1,0:T(8,128)(2,1)}, bf16[384,896]{1,0:T(8,128)(2,1)}, u32[]{:S(2)}, u32[]{:S(2)}) collective-permute-start(bf16[384,896]{1,0:T(8,128)(2,1)} %collective-permute-done.11.refs_13_.refs_14_), channel_id=1, source_target_pairs={{0,1},{1,0},{2,3},{3,2},{4,5},{5,4},{6,7},{7,6},{8,9},{9,8},{10,11... | collective-permute-start | bytes 2064392 | tf_op jit(solution)/shard_map/ppermute | solution.py:21
  69.2 7.2 %collective-permute-start.5 = (bf16[112,1280]{1,0:T(8,128)(2,1)}, bf16[112,1280]{1,0:T(8,128)(2,1)}, u32[]{:S(2)}, u32[]{:S(2)}) collective-permute-start(bf16[112,1280]{1,0:T(8,128)(2,1)} %copy-done.5), channel_id=1, source_target_pairs={{0,56},{8,0},{16,8},{24,16},{32,24},{40,32},{48,40},{56,48},{1,57}... | collective-permute-start | bytes 860168 | tf_op jit(solution)/shard_map/ppermute | solution.py:21
  71.4 7.4 %collective-permute-start.6 = (bf16[112,1280]{1,0:T(8,128)(2,1)}, bf16[112,1280]{1,0:T(8,128)(2,1)}, u32[]{:S(2)}, u32[]{:S(2)}) collective-permute-start(bf16[112,1280]{1,0:T(8,128)(2,1)} %collective-permute-done.4.refs_5_), channel_id=1, source_target_pairs={{0,8},{8,16},{16,24},{24,32},{32,40},{40,48},{48,56},{56,0},{1,9},... | collective-permute-start | bytes 860168 | tf_op jit(solution)/shard_map/ppermute | solution.py:21
  76.3 18.8 %collective-permute-start.17 = (bf16[112,1152]{1,0:T(8,128)(2,1)}, bf16[112,1152]{1,0:T(8,128)(2,1)S(1)}, u32[]{:S(2)}, u32[]{:S(2)}) collective-permute-start(bf16[112,1152]{1,0:T(8,128)(2,1)} %collective-permute-done.15.refs_4_), channel_id=1, source_target_pairs={{0,8},{8,16},{16,24},{24,32},{32,40},{40,48},{48,56},{56,0},{1,9},... | collective-permute-start | bytes 774152 | tf_op jit(solution)/shard_map/ppermute | solution.py:21
  78.9 16.3 %collective-permute-start.19 = (bf16[112,1152]{1,0:T(8,128)(2,1)}, bf16[112,1152]{1,0:T(8,128)(2,1)S(1)}, u32[]{:S(2)}, u32[]{:S(2)}) collective-permute-start(bf16[112,1152]{1,0:T(8,128)(2,1)} %copy-done.9), channel_id=1, source_target_pairs={{0,56},{8,0},{16,8},{24,16},{32,24},{40,32},{48,40},{56,48},{1,57}... | collective-permute-start | bytes 774152 | tf_op jit(solution)/shard_map/ppermute | solution.py:21
  82.0 13.2 %copy-start.8 = (bf16[112,1152]{1,0:T(8,128)(2,1)S(1)}, bf16[112,1152]{1,0:T(8,128)(2,1)}, u32[]{:S(2)}) copy-start(bf16[112,1152]{1,0:T(8,128)(2,1)} %copy-done.7) | copy-start | bytes 774148
  82.0 13.2 %copy-start.10 = (bf16[112,1152]{1,0:T(8,128)(2,1)S(1)}, bf16[112,1152]{1,0:T(8,128)(2,1)}, u32[]{:S(2)}) copy-start(bf16[112,1152]{1,0:T(8,128)(2,1)} %copy-done.9) | copy-start | bytes 774148
  129.3 13.8 %all-to-all-start.2 = ((f32[16,4,256]{2,1,0:T(4,128)}), f32[16,4,256]{2,1,0:T(4,128)S(1)}, u32[]{:S(2)}, u32[]{:S(2)}) async-start(f32[16,4,256]{2,1,0:T(4,128)} %broadcast_in_dim.5), calls=%async_computation.2 | async-start | bytes 131072 | tf_op jit(solution)/shard_map/all_to_all | solution.py:274
  (9 other events, 16.4 us)

commit v2 on v1

--- a/solution.py
+++ b/solution.py
@@ -21,31 +21,39 @@
     return lax.ppermute(x, axis, [(i, (i + by) % size) for i in range(size)])
 
 
-def loss_kernel(place_ref, wanted_ref, *refs, sizes, counts, masked, merged):
+def loss_kernel(place_ref, wanted_ref, *refs, sizes, counts):
     pieces = len(sizes)
-    earlier_ref = refs[0] if merged else None
-    refs = refs[1:] if merged else refs
     inputs = refs[:pieces]
     out_ref, held, weights, logits, top, total, picked, sems = refs[pieces:]
     tokens = wanted_ref.shape[0]
     rows_each = top.shape[0]
     blocks = held.shape[0] // rows_each
-    copies, groups = [], []
-    for count in counts:
-        groups.append(range(len(copies), len(copies) + count))
-        for k in groups[-1]:
-            target = held if len(groups) > 1 else weights
-            start = pl.multiple_of(place_ref[k], 16)
-            copies.append(
-                pltpu.make_async_copy(
-                    inputs[k], target.at[pl.ds(start, sizes[k]), :], sems.at[k]
-                )
-            )
-    for copy in copies:
-        copy.start()
-    limit = place_ref[pieces]
     width_all = weights.shape[1]
     tiles = [min(WIDEST, width_all - at) for at in range(0, width_all, WIDEST)]
+    starts = [sum(tiles[:k]) for k in range(len(tiles))]
+
+    tile_copies, block_copies = [[]], []
+    used = 0
+    for k in range(counts[0]):
+        lo = 0 if inputs[k].shape[1] == WIDTHS[0] else WIDTHS[0]
+        rows = pl.ds(pl.multiple_of(place_ref[k], 16), sizes[k])
+        piece = weights.at[rows, lo : lo + inputs[k].shape[1]]
+        tile_copies[0].append(pltpu.make_async_copy(inputs[k], piece, sems.at[used]))
+        used += 1
+    k = counts[0]
+    for count in counts[1:]:
+        block_copies.append([])
+        for _ in range(count):
+            rows = pl.ds(pl.multiple_of(place_ref[k], 16), sizes[k])
+            block_copies[-1].append(
+                pltpu.make_async_copy(inputs[k], held.at[rows, :], sems.at[used])
+            )
+            used, k = used + 1, k + 1
+    order = [*tile_copies, *block_copies]
+    for group in order:
+        for copy in group:
+            copy.start()
+    limit = place_ref[pieces]
 
     def product(slot, block, at, width):
         rows = held[pl.ds(pl.multiple_of(block * rows_each, 16), rows_each), :]
@@ -62,7 +70,7 @@
             for g in range(0, width, LANES):
                 part = logits[slot, some, g : g + LANES]
                 chosen = jnp.where(wanted == at + g, part, chosen)
-                if at + g >= width_all - masked:
+                if at + g >= width_all - 2 * LANES:
                     lane = lax.broadcasted_iota(jnp.int32, part.shape, 1)
                     part = jnp.where(lane + (at + g) < limit, part, -jnp.inf)
                 parts.append(part)
@@ -92,27 +100,20 @@
             high, chosen = both[0:1, :], both[1:2, :]
             row = place_ref[pieces + 1 + block] + r // tokens
             at = slice(r % tokens, r % tokens + LANES)
-            if merged:
-                before = earlier_ref[row, :, at]
-                joined = jnp.maximum(before, high)
-                high = joined + jnp.log(
-                    jnp.exp(high - joined) + jnp.exp(before - joined)
-                )
-                chosen = chosen + earlier_ref[row + 4, :, at]
             out_ref[row, :, at] = high
             out_ref[row + 4, :, at] = chosen
 
-    starts = [sum(tiles[:k]) for k in range(len(tiles))]
     last = (2, starts[-1], tiles[-1])
 
     def one_block(block, carry):
-        for k, group in enumerate(groups[1:]):
-
-            @pl.when(block == k)
+        def wait(at_block, group):
+            @pl.when(block == at_block)
             def _():
-                for n in group:
-                    copies[n].wait()
-
+                for copy in group:
+                    copy.wait()
+
+        for k, group in enumerate(block_copies):
+            wait(k, group)
         product(0, block, starts[0], tiles[0])
         absorb(*last)
         finish(jnp.maximum(block - 1, 0))
@@ -122,15 +123,65 @@
             absorb((step - 1) % 2, starts[step - 1], tiles[step - 1])
         return carry
 
-    for n in groups[0]:
-        copies[n].wait()
+    for group in tile_copies:
+        for copy in group:
+            copy.wait()
     lax.fori_loop(0, blocks, one_block, 0)
     absorb(*last)
     finish(blocks - 1)
 
 
-def local_stats(depth_pieces, row_blocks, spots, wanted, limit, masked, earlier=()):
-    width = depth_pieces[0][0].shape[-1]
+def join_rows(blocks):
+    count, each, _ = blocks.shape
+    rows = count * each
+
+    def kernel(in_ref, *out_refs):
+        row = lax.broadcasted_iota(jnp.int32, (rows, each), 0)
+        column = lax.broadcasted_iota(jnp.int32, (rows, each), 1)
+        at = 0
+        for out_ref in out_refs:
+            size = out_ref.shape[1]
+            out_ref[...] = sum(
+                jnp.dot(
+                    (row == column + k * each).astype(jnp.bfloat16),
+                    in_ref[k, :, at : at + size],
+                    preferred_element_type=jnp.float32,
+                )
+                for k in range(count)
+            ).astype(jnp.bfloat16)
+            at += size
+
+    vmem = pl.BlockSpec(memory_space=pltpu.VMEM)
+    return pl.pallas_call(
+        kernel,
+        out_shape=[jax.ShapeDtypeStruct((rows, w), jnp.bfloat16) for w in WIDTHS],
+        in_specs=[vmem],
+        out_specs=[vmem] * len(WIDTHS),
+    )(blocks)
+
+
+def join_stats(got, copies):
+    half = got.shape[1] // 2
+
+    def kernel(in_ref, out_ref):
+        parts = in_ref[...]
+        high = jnp.max(parts, axis=0)
+        logs = high + jnp.log(jnp.sum(jnp.exp(parts - high[None]), axis=0))
+        losses = logs[:half] - jnp.sum(parts, axis=0)[half:]
+        for k in range(copies):
+            out_ref[k] = losses
+
+    vmem = pl.BlockSpec(memory_space=pltpu.VMEM)
+    return pl.pallas_call(
+        kernel,
+        out_shape=jax.ShapeDtypeStruct((copies, half, got.shape[2]), jnp.float32),
+        in_specs=[vmem],
+        out_specs=vmem,
+    )(got)
+
+
+def local_stats(depth_pieces, row_blocks, spots, wanted, limit):
+    width = WIDTH
     depth = row_blocks[0][0][0].shape[-1]
     rows_each = sum(a.shape[0] for a, _ in row_blocks[0])
     blocks = len(row_blocks)
@@ -145,9 +196,7 @@
     counts = tuple(len(group) for group in groups)
     state = pltpu.VMEM((rows_each, LANES), jnp.float32)
     return pl.pallas_call(
-        functools.partial(
-            loss_kernel, sizes=sizes, counts=counts, masked=masked, merged=len(earlier)
-        ),
+        functools.partial(loss_kernel, sizes=sizes, counts=counts),
         out_shape=jax.ShapeDtypeStruct(
             (2 * blocks * rows_each // wanted.shape[0], 1, wanted.shape[0]), jnp.float32
         ),
@@ -155,7 +204,6 @@
             pl.BlockSpec(memory_space=pltpu.SMEM),
             pl.BlockSpec(memory_space=pltpu.VMEM),
         ]
-        + [pl.BlockSpec(memory_space=pltpu.VMEM)] * len(earlier)
         + [pl.BlockSpec(memory_space=pl.ANY)] * len(pieces),
         out_specs=pl.BlockSpec(memory_space=pltpu.VMEM),
         scratch_shapes=[
@@ -167,13 +215,13 @@
             state,
             pltpu.SemaphoreType.DMA((len(pieces),)),
         ],
-        compiler_params=pltpu.CompilerParams(vmem_limit_bytes=40 * 2**20),
+        compiler_params=pltpu.CompilerParams(vmem_limit_bytes=58 * 2**20),
         cost_estimate=pl.CostEstimate(
             flops=2 * blocks * rows_each * depth * width,
             bytes_accessed=2 * depth * (blocks * rows_each + width),
             transcendentals=blocks * rows_each * width,
         ),
-    )(place, wanted, *earlier, *pieces)
+    )(place, wanted, *pieces)
 
 
 def covariance(train_losses, query_losses):
@@ -200,8 +248,7 @@
     own = lax.all_to_all(blocks, "x", 0, 0, tiled=True)
     span = nx * depth_each
     depth_pieces = []
-    for half, (at, width) in enumerate(((0, WIDTHS[0]), (WIDTHS[0], WIDTHS[1]))):
-        part = own[:, :, at : at + width].reshape(span, width)
+    for half, part in enumerate(join_rows(own)):
         found = [(part, z * span)]
         up = down = part
         for k in range(1, nz // 2):
@@ -227,7 +274,9 @@
         preferred_element_type=jnp.float32,
     ).astype(jnp.bfloat16)
     mine = lax.dynamic_slice_in_dim(ordered, c * tokens, tokens, 0)
-    mine, _ = lax.optimization_barrier((mine, own))
+    each = TRAIN // (nx * nz)
+    at = (x * nz + z) * each % LANES
+    mine, at, _ = lax.optimization_barrier((mine, at, own))
     left, right = shift(mine, "x", 1), shift(mine, "x", -1)
     row_blocks = [[(ordered, 0)]]
     for rows in (left, right, shift(left, "x", 1)):
@@ -242,15 +291,8 @@
         - lax.broadcasted_iota(jnp.int32, (tokens, LANES), 1)
     )
     limit = jnp.minimum(columns - x * WIDTH, WIDTH).astype(jnp.int32)
-    first = local_stats(depth_pieces[0], row_blocks, spots, wanted, limit, 0)
     stats = local_stats(
-        depth_pieces[1],
-        row_blocks,
-        spots,
-        wanted - WIDTHS[0],
-        limit - WIDTHS[0],
-        256,
-        (first,),
+        depth_pieces[0] + depth_pieces[1], row_blocks, spots, wanted, limit
     ).reshape(nc, 4 * draws, tokens)
 
     sent = jnp.stack(
@@ -264,23 +306,11 @@
     )
     sent = sent.reshape(nx * ny * nc, *sent.shape[3:])
     got = lax.all_to_all(sent, ("x", "y", "c"), 0, 0, tiled=True)
-    logs, chosen = got[:, : 2 * draws], got[:, 2 * draws :]
-    high = jnp.max(logs, axis=0)
-    losses = (
-        high
-        + jnp.log(jnp.sum(jnp.exp(logs - high[None]), axis=0))
-        - jnp.sum(chosen, axis=0)
-    )
     got = lax.all_to_all(
-        jnp.broadcast_to(losses[None], (nz * nc, *losses.shape)),
-        ("z", "c"),
-        0,
-        0,
-        tiled=True,
+        join_stats(got, nz * nc), ("z", "c"), 0, 0, tiled=True
     )
     got = got.reshape(-1, got.shape[-1])
-    each = TRAIN // (nx * nz)
-    mine = lax.dynamic_slice_in_dim(got, (x * nz + z) * each % LANES, each, 1)
+    mine = lax.dynamic_slice_in_dim(got, at, each, 1)
     return covariance(mine, got[:, LANES:])
 
 

time: 145 us -> 136 us (0.938)
  local copies, waits for them, and re-layouts: 12.6 us -> 5.48 us
  starting transfers between devices: 47.2 us -> 41.9 us
  Pallas kernels: 26.3 us -> 30.1 us
    pallas_call x2 -> x3, Pallas kernels: 26.3 us -> 30.1 us  [the longest x1 25.9 us: local_stats(): pl.pallas_call(functools.partial(loss_kernel, sizes=sizes, counts=counts)...]
    slice x2 -> x0, local copies, waits for them, and re-layouts: 2.72 us -> none  [body(): part = own[:, :, at:at + width].reshape(span, width)]
    ppermute x20, starting transfers between devices: 36.3 us -> 33.6 us  [shift(): return lax.ppermute(x, axis, [(i, (i + by) % size) for i in range(size)])]
    all_to_all x1, starting transfers between devices: 6.08 us -> 3.46 us  [body(): got = lax.all_to_all(join_stats(got, nz * nc), ('z', 'c'), 0, 0, tiled=True)]
    unnamed x23 -> x33, local copies, waits for them, and re-layouts: 5.72 us -> 3.43 us
  transfers between devices with their start and end apart: 22 -> 22, of which waited for: 8 -> 10; matrix products, arithmetic and copies ran while one was open for 6% -> 2% of each run, Pallas kernels for 9% -> 2%
where the time goes in v2:
time: 136 us
  starting transfers between devices  41.9 us (31%)
  waiting for transfers between devices  32.7 us (24%)
  Pallas kernels  30.1 us (22%)
  blocking collectives  20.4 us (15%)
  local copies, waits for them, and re-layouts  5.48 us (4%)
  matrix products  2.67 us (2%)
  other arithmetic  1.94 us (1%)
    ppermute x20, starting transfers between devices, shift(): return lax.ppermute(x, axis, [(i, (i + by) % size) for i in range(size)])  33.6 us
    pallas_call x1, Pallas kernels, local_stats(): pl.pallas_call(functools.partial(loss_kernel, sizes=sizes, counts=counts)...  25.9 us
    all_to_all x1, blocking collectives, body(): got = lax.all_to_all(sent, ('x', 'y', 'c'), 0, 0, tiled=True)  20.4 us
    ppermute x20, waiting for transfers between devices, shift(): return lax.ppermute(x, axis, [(i, (i + by) % size) for i in range(size)])  19.4 us
    all_to_all x1, waiting for transfers between devices, body(): got = lax.all_to_all(join_stats(got, nz * nc), ('z', 'c'), 0, 0, tiled=True)  7.82 us
    all_to_all x1, waiting for transfers between devices, body(): own = lax.all_to_all(blocks, 'x', 0, 0, tiled=True)  5.49 us
    all_to_all x1, starting transfers between devices, body(): own = lax.all_to_all(blocks, 'x', 0, 0, tiled=True)  4.83 us
    all_to_all x1, starting transfers between devices, body(): got = lax.all_to_all(join_stats(got, nz * nc), ('z', 'c'), 0, 0, tiled=True)  3.46 us
  transfers between devices with their start and end apart: 22, of which 10 were waited for; matrix products, arithmetic and copies ran while one was open for 2% of the time, Pallas kernels for 2%

profile of v2, /device:TPU:1, one launch (start us, length us, event | category | flops | bytes accessed | tf_op | source)
XLA Modules:
  0.0 135.7 jit_solution(1767477681989884667)
XLA Ops:
  2.2 4.8 %all-to-all-start = ((bf16[4,28,2432]{2,1,0:T(8,128)(2,1)}), bf16[4,28,2432]{2,1,0:T(8,128)(2,1)S(1)}, u32[]{:S(2)}, u32[]{:S(2)}) async-start(bf16[4,28,2432]{2,1,0:T(8,128)(2,1)} %pad_maximum_fusion), calls=%async_computation | async-start | bytes 1245184 | tf_op jit(solution)/shard_map/all_to_all | solution.py:248
  7.1 1.8 %fusion.1 = bf16[896,768]{0,1:T(8,128)(2,1)S(1)} fusion(bf16[768,896]{1,0:T(8,128)(2,1)S(1)} %bitcast.40, s32[896]{0:T(1024)S(1)} %fusion.18), kind=kOutput, calls=%fused_computation.2 | convolution fusion | flops 1234616320 | bytes 2756096 | tf_op jit(solution)/shard_map/dot_general | solution.py:271
  10.1 5.5 %all-to-all-done.in_ref = bf16[4,28,2432]{2,1,0:T(8,128)(2,1)S(1)} async-done(((bf16[4,28,2432]{2,1,0:T(8,128)(2,1)}), bf16[4,28,2432]{2,1,0:T(8,128)(2,1)S(1)}, u32[]{:S(2)}, u32[]{:S(2)}) %all-to-all-start) | async-done | bytes 544800 | tf_op jit(solution)/shard_map/all_to_all | solution.py:248
  16.4 2.5 %shard_map.37 = (bf16[112,1280]{1,0:T(8,128)(2,1)}, bf16[112,1152]{1,0:T(8,128)(2,1)}) custom-call(bf16[4,28,2432]{2,1,0:T(8,128)(2,1)} %copy-done.1), custom_call_target="tpu_custom_call" | custom-call | tf_op jit(solution)/shard_map/pallas_call | solution.py:155
  19.0 6.7 %collective-permute-start.8 = (bf16[112,1152]{1,0:T(8,128)(2,1)}, bf16[112,1152]{1,0:T(8,128)(2,1)S(1)}, u32[]{:S(2)}, u32[]{:S(2)}) collective-permute-start(bf16[112,1152]{1,0:T(8,128)(2,1)} %get-tuple-element.10.refs_8_), channel_id=1, source_target_pairs={{0,56},{8,0},{16,8},{24,16},{32,24},{40,32},{48,40},{56,48},{1,57}... | collective-permute-start | bytes 774152 | tf_op jit(solution)/shard_map/ppermute | solution.py:21
  25.7 2.7 %collective-permute-start.1 = (bf16[112,1280]{1,0:T(8,128)(2,1)}, bf16[112,1280]{1,0:T(8,128)(2,1)S(1)}, u32[]{:S(2)}, u32[]{:S(2)}) collective-permute-start(bf16[112,1280]{1,0:T(8,128)(2,1)} %get-tuple-element.9.refs_0_), channel_id=1, source_target_pairs={{0,56},{8,0},{16,8},{24,16},{32,24},{40,32},{48,40},{56,48},{1,57}... | collective-permute-start | bytes 860168 | tf_op jit(solution)/shard_map/ppermute | solution.py:21
  28.4 1.4 %collective-permute-done.8.refs_10_ = bf16[112,1152]{1,0:T(8,128)(2,1)S(1)} collective-permute-done((bf16[112,1152]{1,0:T(8,128)(2,1)}, bf16[112,1152]{1,0:T(8,128)(2,1)S(1)}, u32[]{:S(2)}, u32[]{:S(2)}) %collective-permute-start.8) | collective-permute-done | bytes 258080 | tf_op jit(solution)/shard_map/ppermute | solution.py:21
  29.8 1.6 %collective-permute-start.16 = (bf16[384,896]{1,0:T(8,128)(2,1)S(1)}, bf16[384,896]{1,0:T(8,128)(2,1)}, u32[]{:S(2)}, u32[]{:S(2)}) collective-permute-start(bf16[384,896]{1,0:T(8,128)(2,1)S(1)} %dynamic-slice_bitcast_fusion), channel_id=1, source_target_pairs={{0,192},{64,0},{128,64},{192,128},{1,193},{65,1},{129,65},{193,129... | collective-permute-start | bytes 2064392 | tf_op jit(solution)/shard_map/ppermute | solution.py:21
  31.4 1.4 %collective-permute-done.7.refs_9_ = bf16[112,1152]{1,0:T(8,128)(2,1)S(1)} collective-permute-done((bf16[112,1152]{1,0:T(8,128)(2,1)}, bf16[112,1152]{1,0:T(8,128)(2,1)S(1)}, u32[]{:S(2)}, u32[]{:S(2)}) %collective-permute-start.7) | collective-permute-done | bytes 258080 | tf_op jit(solution)/shard_map/ppermute | solution.py:21
  32.8 6.0 %collective-permute-start.10 = (bf16[112,1152]{1,0:T(8,128)(2,1)S(1)}, bf16[112,1152]{1,0:T(8,128)(2,1)S(1)}, u32[]{:S(2)}, u32[]{:S(2)}) collective-permute-start(bf16[112,1152]{1,0:T(8,128)(2,1)S(1)} %collective-permute-done.8.refs_10_), channel_id=1, source_target_pairs={{0,56},{8,0},{16,8},{24,16},{32,24},{40,32},{48,40},{56,48},{1,57}... | collective-permute-start | bytes 774152 | tf_op jit(solution)/shard_map/ppermute | solution.py:21
  40.3 1.8 %collective-permute-done.10.refs_12_ = bf16[112,1152]{1,0:T(8,128)(2,1)S(1)} collective-permute-done((bf16[112,1152]{1,0:T(8,128)(2,1)S(1)}, bf16[112,1152]{1,0:T(8,128)(2,1)S(1)}, u32[]{:S(2)}, u32[]{:S(2)}) %collective-permute-start.10) | collective-permute-done | bytes 258080 | tf_op jit(solution)/shard_map/ppermute | solution.py:21
  42.1 4.3 %collective-permute-done.9.refs_11_ = bf16[112,1152]{1,0:T(8,128)(2,1)S(1)} collective-permute-done((bf16[112,1152]{1,0:T(8,128)(2,1)S(1)}, bf16[112,1152]{1,0:T(8,128)(2,1)S(1)}, u32[]{:S(2)}, u32[]{:S(2)}) %collective-permute-start.9) | collective-permute-done | bytes 258080 | tf_op jit(solution)/shard_map/ppermute | solution.py:21
  46.4 1.5 %collective-permute-done.3.refs_4_ = bf16[112,1280]{1,0:T(8,128)(2,1)} collective-permute-done((bf16[112,1280]{1,0:T(8,128)(2,1)S(1)}, bf16[112,1280]{1,0:T(8,128)(2,1)}, u32[]{:S(2)}, u32[]{:S(2)}) %collective-permute-start.3) | collective-permute-done | bytes 286752 | tf_op jit(solution)/shard_map/ppermute | solution.py:21
  47.9 4.0 %collective-permute-done.2.refs_3_ = bf16[112,1280]{1,0:T(8,128)(2,1)} collective-permute-done((bf16[112,1280]{1,0:T(8,128)(2,1)S(1)}, bf16[112,1280]{1,0:T(8,128)(2,1)}, u32[]{:S(2)}, u32[]{:S(2)}) %collective-permute-start.2) | collective-permute-done | bytes 286752 | tf_op jit(solution)/shard_map/ppermute | solution.py:21
  53.4 8.6 %collective-permute-start.15 = (bf16[384,896]{1,0:T(8,128)(2,1)S(1)}, bf16[384,896]{1,0:T(8,128)(2,1)S(1)}, u32[]{:S(2)}, u32[]{:S(2)}) collective-permute-start(bf16[384,896]{1,0:T(8,128)(2,1)S(1)} %collective-permute-done.14.refs_17_), channel_id=1, source_target_pairs={{0,1},{1,0},{2,3},{3,2},{4,5},{5,4},{6,7},{7,6},{8,9},{9,8},{10,11... | collective-permute-start | bytes 2064392 | tf_op jit(solution)/shard_map/ppermute | solution.py:21
  62.0 2.7 %collective-permute-start.17 = (bf16[384,896]{1,0:T(8,128)(2,1)}, bf16[384,896]{1,0:T(8,128)(2,1)}, u32[]{:S(2)}, u32[]{:S(2)}) collective-permute-start(bf16[384,896]{1,0:T(8,128)(2,1)} %collective-permute-done.16.refs_19_), channel_id=1, source_target_pairs={{0,1},{1,0},{2,3},{3,2},{4,5},{5,4},{6,7},{7,6},{8,9},{9,8},{10,11... | collective-permute-start | bytes 2064392 | tf_op jit(solution)/shard_map/ppermute | solution.py:21
  65.4 1.5 %collective-permute-start.13 = (bf16[112,1152]{1,0:T(8,128)(2,1)}, bf16[112,1152]{1,0:T(8,128)(2,1)}, u32[]{:S(2)}, u32[]{:S(2)}) collective-permute-start(bf16[112,1152]{1,0:T(8,128)(2,1)} %copy-done.14), channel_id=1, source_target_pairs={{0,56},{8,0},{16,8},{24,16},{32,24},{40,32},{48,40},{56,48},{1,57}... | collective-permute-start | bytes 774152 | tf_op jit(solution)/shard_map/ppermute | solution.py:21
  68.6 3.5 %collective-permute-done.13.refs_15_ = bf16[112,1152]{1,0:T(8,128)(2,1)} collective-permute-done((bf16[112,1152]{1,0:T(8,128)(2,1)}, bf16[112,1152]{1,0:T(8,128)(2,1)}, u32[]{:S(2)}, u32[]{:S(2)}) %collective-permute-start.13) | collective-permute-done | bytes 258080 | tf_op jit(solution)/shard_map/ppermute | solution.py:21
  72.1 1.5 %collective-permute-done.6.refs_7_ = bf16[112,1280]{1,0:T(8,128)(2,1)S(1)} collective-permute-done((bf16[112,1280]{1,0:T(8,128)(2,1)S(1)}, bf16[112,1280]{1,0:T(8,128)(2,1)S(1)}, u32[]{:S(2)}, u32[]{:S(2)}) %collective-permute-start.6) | collective-permute-done | bytes 286752 | tf_op jit(solution)/shard_map/ppermute | solution.py:21
  74.6 25.9 %shard_map.38 = f32[16,1,384]{2,1,0:T(1,128)} custom-call(s32[28]{0:T(128)} %stack.111.place_ref, s32[384,128]{1,0:T(8,128)} %iota_subtract_fusion.wanted_ref, bf16[112,1280]{1,0:T(8,128)(2,1)} %get-tuple-element.9.refs_0_, bf16[112,1280]{1,0:T(8,128)(2,1)} %copy-done.7, bf16[112,1280]{1,0:T(8,128)(2,1)} %copy-done.6, ...), custom_call_target="tpu_custom_call" | custom-call | flops 13388218368 | bytes 9863168 | tf_op jit(solution)/shard_map/pallas_call | solution.py:198
  101.3 20.4 %all_to_all.15.in_ref = f32[32,8,256]{2,1,0:T(8,128)} all-to-all(f32[32,8,256]{2,1,0:T(8,128)S(1)} %bitcast.41), channel_id=1, replica_groups=mesh['x'=4,'z'=8,'y'=4,'c'=2] {'x','y','c'}, dimensions={0} | all-to-all | bytes 524288 | tf_op jit(solution)/shard_map/all_to_all | solution.py:308
  121.7 1.7 %shard_map.39 = f32[16,4,256]{2,1,0:T(4,128)} custom-call(f32[32,8,256]{2,1,0:T(8,128)} %all_to_all.15.in_ref), custom_call_target="tpu_custom_call" | custom-call | tf_op jit(solution)/shard_map/pallas_call | solution.py:175
  123.4 3.5 %all-to-all-start.2 = ((f32[16,4,256]{2,1,0:T(4,128)}), f32[16,4,256]{2,1,0:T(4,128)S(1)}, u32[]{:S(2)}, u32[]{:S(2)}) async-start(f32[16,4,256]{2,1,0:T(4,128)} %shard_map.39), calls=%async_computation.2 | async-start | bytes 131072 | tf_op jit(solution)/shard_map/all_to_all | solution.py:309
  126.8 7.8 %all-to-all-done.2 = f32[16,4,256]{2,1,0:T(4,128)S(1)} async-done(((f32[16,4,256]{2,1,0:T(4,128)}), f32[16,4,256]{2,1,0:T(4,128)S(1)}, u32[]{:S(2)}, u32[]{:S(2)}) %all-to-all-start.2) | async-done | bytes 65568 | tf_op jit(solution)/shard_map/all_to_all | solution.py:309
  (75 shorter events, 12.3 us)
Async XLA Ops:
  2.2 13.3 %all-to-all-start = ((bf16[4,28,2432]{2,1,0:T(8,128)(2,1)}), bf16[4,28,2432]{2,1,0:T(8,128)(2,1)S(1)}, u32[]{:S(2)}, u32[]{:S(2)}) async-start(bf16[4,28,2432]{2,1,0:T(8,128)(2,1)} %pad_maximum_fusion), calls=%async_computation | async-start | bytes 1245184 | tf_op jit(solution)/shard_map/all_to_all | solution.py:248
  10.0 56.8 %copy-start.3 = (s32[384]{0:T(512)S(1)}, s32[384]{0:T(512)}, u32[]{:S(2)}) copy-start(s32[384]{0:T(512)} %param.5) | copy-start | bytes 4612
  15.6 15.8 %collective-permute-start.14 = (bf16[384,896]{1,0:T(8,128)(2,1)S(1)}, bf16[384,896]{1,0:T(8,128)(2,1)S(1)}, u32[]{:S(2)}, u32[]{:S(2)}) collective-permute-start(bf16[384,896]{1,0:T(8,128)(2,1)S(1)} %dynamic-slice_bitcast_fusion), channel_id=1, source_target_pairs={{0,64},{64,128},{128,192},{192,0},{1,65},{65,129},{129,193},{193,1... | collective-permute-start | bytes 2064392 | tf_op jit(solution)/shard_map/ppermute | solution.py:21
  19.0 10.8 %collective-permute-start.8 = (bf16[112,1152]{1,0:T(8,128)(2,1)}, bf16[112,1152]{1,0:T(8,128)(2,1)S(1)}, u32[]{:S(2)}, u32[]{:S(2)}) collective-permute-start(bf16[112,1152]{1,0:T(8,128)(2,1)} %get-tuple-element.10.refs_8_), channel_id=1, source_target_pairs={{0,56},{8,0},{16,8},{24,16},{32,24},{40,32},{48,40},{56,48},{1,57}... | collective-permute-start | bytes 774152 | tf_op jit(solution)/shard_map/ppermute | solution.py:21
  25.7 7.1 %collective-permute-start.7 = (bf16[112,1152]{1,0:T(8,128)(2,1)}, bf16[112,1152]{1,0:T(8,128)(2,1)S(1)}, u32[]{:S(2)}, u32[]{:S(2)}) collective-permute-start(bf16[112,1152]{1,0:T(8,128)(2,1)} %get-tuple-element.10.refs_8_), channel_id=1, source_target_pairs={{0,8},{8,16},{16,24},{24,32},{32,40},{40,48},{48,56},{56,0},{1,9},... | collective-permute-start | bytes 774152 | tf_op jit(solution)/shard_map/ppermute | solution.py:21
  25.7 13.1 %collective-permute-start.1 = (bf16[112,1280]{1,0:T(8,128)(2,1)}, bf16[112,1280]{1,0:T(8,128)(2,1)S(1)}, u32[]{:S(2)}, u32[]{:S(2)}) collective-permute-start(bf16[112,1280]{1,0:T(8,128)(2,1)} %get-tuple-element.9.refs_0_), channel_id=1, source_target_pairs={{0,56},{8,0},{16,8},{24,16},{32,24},{40,32},{48,40},{56,48},{1,57}... | collective-permute-start | bytes 860168 | tf_op jit(solution)/shard_map/ppermute | solution.py:21
  28.4 11.2 %collective-permute-start = (bf16[112,1280]{1,0:T(8,128)(2,1)}, bf16[112,1280]{1,0:T(8,128)(2,1)S(1)}, u32[]{:S(2)}, u32[]{:S(2)}) collective-permute-start(bf16[112,1280]{1,0:T(8,128)(2,1)} %get-tuple-element.9.refs_0_), channel_id=1, source_target_pairs={{0,8},{8,16},{16,24},{24,32},{32,40},{40,48},{48,56},{56,0},{1,9},... | collective-permute-start | bytes 860168 | tf_op jit(solution)/shard_map/ppermute | solution.py:21
  29.8 22.9 %collective-permute-start.16 = (bf16[384,896]{1,0:T(8,128)(2,1)S(1)}, bf16[384,896]{1,0:T(8,128)(2,1)}, u32[]{:S(2)}, u32[]{:S(2)}) collective-permute-start(bf16[384,896]{1,0:T(8,128)(2,1)S(1)} %dynamic-slice_bitcast_fusion), channel_id=1, source_target_pairs={{0,192},{64,0},{128,64},{192,128},{1,193},{65,1},{129,65},{193,129... | collective-permute-start | bytes 2064392 | tf_op jit(solution)/shard_map/ppermute | solution.py:21
  31.4 42.2 %copy-start.4 = (bf16[384,896]{1,0:T(8,128)(2,1)}, bf16[384,896]{1,0:T(8,128)(2,1)S(1)}, u32[]{:S(2)}) copy-start(bf16[384,896]{1,0:T(8,128)(2,1)S(1)} %collective-permute-done.14.refs_17_) | copy-start | bytes 2064388
  31.4 33.4 %collective-permute-start.18 = (bf16[384,896]{1,0:T(8,128)(2,1)S(1)}, bf16[384,896]{1,0:T(8,128)(2,1)}, u32[]{:S(2)}, u32[]{:S(2)}) collective-permute-start(bf16[384,896]{1,0:T(8,128)(2,1)S(1)} %collective-permute-done.14.refs_17_), channel_id=1, source_target_pairs={{0,64},{64,128},{128,192},{192,0},{1,65},{65,129},{129,193},{193,1... | collective-permute-start | bytes 2064392 | tf_op jit(solution)/shard_map/ppermute | solution.py:21
  32.8 9.3 %collective-permute-start.10 = (bf16[112,1152]{1,0:T(8,128)(2,1)S(1)}, bf16[112,1152]{1,0:T(8,128)(2,1)S(1)}, u32[]{:S(2)}, u32[]{:S(2)}) collective-permute-start(bf16[112,1152]{1,0:T(8,128)(2,1)S(1)} %collective-permute-done.8.refs_10_), channel_id=1, source_target_pairs={{0,56},{8,0},{16,8},{24,16},{32,24},{40,32},{48,40},{56,48},{1,57}... | collective-permute-start | bytes 774152 | tf_op jit(solution)/shard_map/ppermute | solution.py:21
  38.8 9.1 %collective-permute-start.3 = (bf16[112,1280]{1,0:T(8,128)(2,1)S(1)}, bf16[112,1280]{1,0:T(8,128)(2,1)}, u32[]{:S(2)}, u32[]{:S(2)}) collective-permute-start(bf16[112,1280]{1,0:T(8,128)(2,1)S(1)} %collective-permute-done.1.refs_2_), channel_id=1, source_target_pairs={{0,56},{8,0},{16,8},{24,16},{32,24},{40,32},{48,40},{56,48},{1,57}... | collective-permute-start | bytes 860168 | tf_op jit(solution)/shard_map/ppermute | solution.py:21
  39.6 6.8 %collective-permute-start.9 = (bf16[112,1152]{1,0:T(8,128)(2,1)S(1)}, bf16[112,1152]{1,0:T(8,128)(2,1)S(1)}, u32[]{:S(2)}, u32[]{:S(2)}) collective-permute-start(bf16[112,1152]{1,0:T(8,128)(2,1)S(1)} %collective-permute-done.7.refs_9_), channel_id=1, source_target_pairs={{0,8},{8,16},{16,24},{24,32},{32,40},{40,48},{48,56},{56,0},{1,9},... | collective-permute-start | bytes 774152 | tf_op jit(solution)/shard_map/ppermute | solution.py:21
  42.1 9.8 %collective-permute-start.2 = (bf16[112,1280]{1,0:T(8,128)(2,1)S(1)}, bf16[112,1280]{1,0:T(8,128)(2,1)}, u32[]{:S(2)}, u32[]{:S(2)}) collective-permute-start(bf16[112,1280]{1,0:T(8,128)(2,1)S(1)} %collective-permute-done.refs_1_), channel_id=1, source_target_pairs={{0,8},{8,16},{16,24},{24,32},{32,40},{40,48},{48,56},{56,0},{1,9},... | collective-permute-start | bytes 860168 | tf_op jit(solution)/shard_map/ppermute | solution.py:21
  46.4 7.1 %collective-permute-start.12 = (bf16[112,1152]{1,0:T(8,128)(2,1)S(1)}, bf16[112,1152]{1,0:T(8,128)(2,1)S(1)}, u32[]{:S(2)}, u32[]{:S(2)}) collective-permute-start(bf16[112,1152]{1,0:T(8,128)(2,1)S(1)} %collective-permute-done.10.refs_12_), channel_id=1, source_target_pairs={{0,56},{8,0},{16,8},{24,16},{32,24},{40,32},{48,40},{56,48},{1,57}... | collective-permute-start | bytes 774152 | tf_op jit(solution)/shard_map/ppermute | solution.py:21
  47.9 14.1 %collective-permute-start.11 = (bf16[112,1152]{1,0:T(8,128)(2,1)S(1)}, bf16[112,1152]{1,0:T(8,128)(2,1)S(1)}, u32[]{:S(2)}, u32[]{:S(2)}) collective-permute-start(bf16[112,1152]{1,0:T(8,128)(2,1)S(1)} %collective-permute-done.9.refs_11_), channel_id=1, source_target_pairs={{0,8},{8,16},{16,24},{24,32},{32,40},{40,48},{48,56},{56,0},{1,9},... | collective-permute-start | bytes 774152 | tf_op jit(solution)/shard_map/ppermute | solution.py:21
  51.9 13.5 %collective-permute-start.5 = (bf16[112,1280]{1,0:T(8,128)(2,1)}, bf16[112,1280]{1,0:T(8,128)(2,1)}, u32[]{:S(2)}, u32[]{:S(2)}) collective-permute-start(bf16[112,1280]{1,0:T(8,128)(2,1)} %collective-permute-done.3.refs_4_), channel_id=1, source_target_pairs={{0,56},{8,0},{16,8},{24,16},{32,24},{40,32},{48,40},{56,48},{1,57}... | collective-permute-start | bytes 860168 | tf_op jit(solution)/shard_map/ppermute | solution.py:21
  52.6 14.2 %collective-permute-start.4 = (bf16[112,1280]{1,0:T(8,128)(2,1)}, bf16[112,1280]{1,0:T(8,128)(2,1)S(1)}, u32[]{:S(2)}, u32[]{:S(2)}) collective-permute-start(bf16[112,1280]{1,0:T(8,128)(2,1)} %collective-permute-done.2.refs_3_), channel_id=1, source_target_pairs={{0,8},{8,16},{16,24},{24,32},{32,40},{40,48},{48,56},{56,0},{1,9},... | collective-permute-start | bytes 860168 | tf_op jit(solution)/shard_map/ppermute | solution.py:21
  53.4 20.2 %collective-permute-start.15 = (bf16[384,896]{1,0:T(8,128)(2,1)S(1)}, bf16[384,896]{1,0:T(8,128)(2,1)S(1)}, u32[]{:S(2)}, u32[]{:S(2)}) collective-permute-start(bf16[384,896]{1,0:T(8,128)(2,1)S(1)} %collective-permute-done.14.refs_17_), channel_id=1, source_target_pairs={{0,1},{1,0},{2,3},{3,2},{4,5},{5,4},{6,7},{7,6},{8,9},{9,8},{10,11... | collective-permute-start | bytes 2064392 | tf_op jit(solution)/shard_map/ppermute | solution.py:21
  62.0 11.6 %collective-permute-start.17 = (bf16[384,896]{1,0:T(8,128)(2,1)}, bf16[384,896]{1,0:T(8,128)(2,1)}, u32[]{:S(2)}, u32[]{:S(2)}) collective-permute-start(bf16[384,896]{1,0:T(8,128)(2,1)} %collective-permute-done.16.refs_19_), channel_id=1, source_target_pairs={{0,1},{1,0},{2,3},{3,2},{4,5},{5,4},{6,7},{7,6},{8,9},{9,8},{10,11... | collective-permute-start | bytes 2064392 | tf_op jit(solution)/shard_map/ppermute | solution.py:21
  64.8 8.8 %collective-permute-start.19 = (bf16[384,896]{1,0:T(8,128)(2,1)}, bf16[384,896]{1,0:T(8,128)(2,1)}, u32[]{:S(2)}, u32[]{:S(2)}) collective-permute-start(bf16[384,896]{1,0:T(8,128)(2,1)} %collective-permute-done.18.refs_21_), channel_id=1, source_target_pairs={{0,1},{1,0},{2,3},{3,2},{4,5},{5,4},{6,7},{7,6},{8,9},{9,8},{10,11... | collective-permute-start | bytes 2064392 | tf_op jit(solution)/shard_map/ppermute | solution.py:21
  65.4 6.7 %collective-permute-start.13 = (bf16[112,1152]{1,0:T(8,128)(2,1)}, bf16[112,1152]{1,0:T(8,128)(2,1)}, u32[]{:S(2)}, u32[]{:S(2)}) collective-permute-start(bf16[112,1152]{1,0:T(8,128)(2,1)} %copy-done.14), channel_id=1, source_target_pairs={{0,56},{8,0},{16,8},{24,16},{32,24},{40,32},{48,40},{56,48},{1,57}... | collective-permute-start | bytes 774152 | tf_op jit(solution)/shard_map/ppermute | solution.py:21
  66.9 6.7 %collective-permute-start.6 = (bf16[112,1280]{1,0:T(8,128)(2,1)S(1)}, bf16[112,1280]{1,0:T(8,128)(2,1)S(1)}, u32[]{:S(2)}, u32[]{:S(2)}) collective-permute-start(bf16[112,1280]{1,0:T(8,128)(2,1)S(1)} %collective-permute-done.4.refs_5_), channel_id=1, source_target_pairs={{0,8},{8,16},{16,24},{24,32},{32,40},{40,48},{48,56},{56,0},{1,9},... | collective-permute-start | bytes 860168 | tf_op jit(solution)/shard_map/ppermute | solution.py:21
  123.4 11.3 %all-to-all-start.2 = ((f32[16,4,256]{2,1,0:T(4,128)}), f32[16,4,256]{2,1,0:T(4,128)S(1)}, u32[]{:S(2)}, u32[]{:S(2)}) async-start(f32[16,4,256]{2,1,0:T(4,128)} %shard_map.39), calls=%async_computation.2 | async-start | bytes 131072 | tf_op jit(solution)/shard_map/all_to_all | solution.py:309
  (14 other events, 167.9 us)

commit v3 on v2

--- a/solution.py
+++ b/solution.py
@@ -12,7 +12,7 @@
 LANES = 128
 WIDTHS = (1280, 1152)
 WIDTH = sum(WIDTHS)
-WIDEST = 512
+WIDEST = 1280
 CHUNK = 32
 
 
@@ -24,7 +24,7 @@
 def loss_kernel(place_ref, wanted_ref, *refs, sizes, counts):
     pieces = len(sizes)
     inputs = refs[:pieces]
-    out_ref, held, weights, logits, top, total, picked, sems = refs[pieces:]
+    out_ref, rows_ref, held, weights, logits, top, total, picked, sems = refs[pieces:]
     tokens = wanted_ref.shape[0]
     rows_each = top.shape[0]
     blocks = held.shape[0] // rows_each
@@ -100,8 +100,8 @@
             high, chosen = both[0:1, :], both[1:2, :]
             row = place_ref[pieces + 1 + block] + r // tokens
             at = slice(r % tokens, r % tokens + LANES)
-            out_ref[row, :, at] = high
-            out_ref[row + 4, :, at] = chosen
+            rows_ref[row, :, at] = high
+            rows_ref[row + 4, :, at] = chosen
 
     last = (2, starts[-1], tiles[-1])
 
@@ -129,25 +129,61 @@
     lax.fori_loop(0, blocks, one_block, 0)
     absorb(*last)
     finish(blocks - 1)
+    receivers, each, _ = out_ref.shape
+    for core in range(2):
+        rows = [rows_ref[core * each + k] for k in range(each)]
+        rows = jnp.concatenate(rows, axis=0)
+        for group in range(TRAIN // LANES):
+            part = rows[:, group * LANES : (group + 1) * LANES]
+            part = jnp.concatenate([part, rows[:, TRAIN:]], axis=1)
+            members = receivers * LANES // TRAIN
+            for k in range(group * members + core, (group + 1) * members, 2):
+                out_ref[k] = part
+
+
+def cut_columns(matrix, count):
+    rows, columns = matrix.shape
+
+    def kernel(in_ref, out_ref):
+        for k in range(count):
+            size = min(WIDTH, columns - k * WIDTH)
+            if size < WIDTH:
+                out_ref[k] = jnp.zeros((rows, WIDTH), jnp.bfloat16)
+            out_ref[k, :, :size] = in_ref[:, k * WIDTH : k * WIDTH + size]
+
+    vmem = pl.BlockSpec(memory_space=pltpu.VMEM)
+    return pl.pallas_call(
+        kernel,
+        out_shape=jax.ShapeDtypeStruct((count, rows, WIDTH), jnp.bfloat16),
+        in_specs=[vmem],
+        out_specs=vmem,
+    )(matrix)
 
 
 def join_rows(blocks):
-    count, each, _ = blocks.shape
-    rows = count * each
-
-    def kernel(in_ref, *out_refs):
-        row = lax.broadcasted_iota(jnp.int32, (rows, each), 0)
-        column = lax.broadcasted_iota(jnp.int32, (rows, each), 1)
+    count, each, width = blocks.shape
+    rows, slot = count * each, 32
+
+    def kernel(in_ref, *refs):
+        *out_refs, apart = refs
+        row = lax.broadcasted_iota(jnp.int32, (rows, count * slot), 0)
+        column = lax.broadcasted_iota(jnp.int32, (rows, count * slot), 1)
+        chooser = sum(
+            (
+                (column - k * slot == row - k * each)
+                & (column >= k * slot)
+                & (column < k * slot + each)
+            ).astype(jnp.float32)
+            for k in range(count)
+        ).astype(jnp.bfloat16)
+        apart[...] = jnp.zeros_like(apart)
+        for k in range(count):
+            apart[k * slot : k * slot + each, :] = in_ref[k]
         at = 0
         for out_ref in out_refs:
             size = out_ref.shape[1]
-            out_ref[...] = sum(
-                jnp.dot(
-                    (row == column + k * each).astype(jnp.bfloat16),
-                    in_ref[k, :, at : at + size],
-                    preferred_element_type=jnp.float32,
-                )
-                for k in range(count)
+            out_ref[...] = jnp.dot(
+                chooser, apart[:, at : at + size], preferred_element_type=jnp.float32
             ).astype(jnp.bfloat16)
             at += size
 
@@ -157,6 +193,7 @@
         out_shape=[jax.ShapeDtypeStruct((rows, w), jnp.bfloat16) for w in WIDTHS],
         in_specs=[vmem],
         out_specs=[vmem] * len(WIDTHS),
+        scratch_shapes=[pltpu.VMEM((count * slot, width), jnp.bfloat16)],
     )(blocks)
 
 
@@ -180,25 +217,22 @@
     )(got)
 
 
-def local_stats(depth_pieces, row_blocks, spots, wanted, limit):
+def local_stats(depth_pieces, row_blocks, place, wanted, receivers):
     width = WIDTH
-    depth = row_blocks[0][0][0].shape[-1]
-    rows_each = sum(a.shape[0] for a, _ in row_blocks[0])
+    depth = row_blocks[0][0].shape[-1]
+    rows_each = sum(a.shape[0] for a in row_blocks[0])
     blocks = len(row_blocks)
-    groups = [list(depth_pieces)] + [
-        [(a, k * rows_each + at) for a, at in block]
-        for k, block in enumerate(row_blocks)
-    ]
-    everything = [piece for group in groups for piece in group]
-    place = jnp.stack([jnp.asarray(s, jnp.int32) for _, s in everything] + [limit] + spots)
-    pieces = [a for a, _ in everything]
+    tokens = wanted.shape[0]
+    rows_total = blocks * rows_each
+    groups = [list(depth_pieces), *row_blocks]
+    pieces = [piece for group in groups for piece in group]
     sizes = tuple(a.shape[0] for a in pieces)
     counts = tuple(len(group) for group in groups)
     state = pltpu.VMEM((rows_each, LANES), jnp.float32)
     return pl.pallas_call(
         functools.partial(loss_kernel, sizes=sizes, counts=counts),
         out_shape=jax.ShapeDtypeStruct(
-            (2 * blocks * rows_each // wanted.shape[0], 1, wanted.shape[0]), jnp.float32
+            (receivers, rows_total // tokens, tokens - TRAIN + LANES), jnp.float32
         ),
         in_specs=[
             pl.BlockSpec(memory_space=pltpu.SMEM),
@@ -207,7 +241,8 @@
         + [pl.BlockSpec(memory_space=pl.ANY)] * len(pieces),
         out_specs=pl.BlockSpec(memory_space=pltpu.VMEM),
         scratch_shapes=[
-            pltpu.VMEM((blocks * rows_each, depth), jnp.bfloat16),
+            pltpu.VMEM((2 * rows_total // tokens, 1, tokens), jnp.float32),
+            pltpu.VMEM((rows_total, depth), jnp.bfloat16),
             pltpu.VMEM((depth, width), jnp.bfloat16),
             pltpu.VMEM((3, rows_each, WIDEST), jnp.float32),
             state,
@@ -215,7 +250,7 @@
             state,
             pltpu.SemaphoreType.DMA((len(pieces),)),
         ],
-        compiler_params=pltpu.CompilerParams(vmem_limit_bytes=58 * 2**20),
+        compiler_params=pltpu.CompilerParams(vmem_limit_bytes=36 * 2**20),
         cost_estimate=pl.CostEstimate(
             flops=2 * blocks * rows_each * depth * width,
             bytes_accessed=2 * depth * (blocks * rows_each + width),
@@ -243,23 +278,9 @@
     ny, nc = lax.axis_size("y"), lax.axis_size("c")
     x, z, y, c = (lax.axis_index(name) for name in ("x", "z", "y", "c"))
 
-    padded = jnp.pad(unembed, ((0, 0), (0, nx * WIDTH - columns)))
-    blocks = jnp.stack([padded[:, k * WIDTH : (k + 1) * WIDTH] for k in range(nx)])
+    span = nx * depth_each
+    blocks = cut_columns(unembed, nx)
     own = lax.all_to_all(blocks, "x", 0, 0, tiled=True)
-    span = nx * depth_each
-    depth_pieces = []
-    for half, part in enumerate(join_rows(own)):
-        found = [(part, z * span)]
-        up = down = part
-        for k in range(1, nz // 2):
-            up = shift(up, "z", 1)
-            down = shift(down, "z", -1)
-            found.append((up, (z + nz - k) % nz * span))
-            found.append((down, (z + k) % nz * span))
-        far = (up, 1) if not half else (down, -1)
-        far = shift(far[0], "z", far[1])
-        found.append((far, (z + nz // 2) % nz * span))
-        depth_pieces.append(found)
 
     source = jnp.arange(model_width, dtype=jnp.int32)
     zp, rest = source // span, source % span
@@ -274,43 +295,56 @@
         preferred_element_type=jnp.float32,
     ).astype(jnp.bfloat16)
     mine = lax.dynamic_slice_in_dim(ordered, c * tokens, tokens, 0)
-    each = TRAIN // (nx * nz)
-    at = (x * nz + z) * each % LANES
-    mine, at, _ = lax.optimization_barrier((mine, at, own))
-    left, right = shift(mine, "x", 1), shift(mine, "x", -1)
-    row_blocks = [[(ordered, 0)]]
-    for rows in (left, right, shift(left, "x", 1)):
-        row_blocks.append([(rows, c * tokens), (shift(rows, "c", 1), (1 - c) * tokens)])
-    spots = [(x + k) % nx for k in (0, nx - 1, 1, 2)]
-    spots = [at // nc * (4 * draws) + at % nc * draws for at in spots]
-
+
+    steps = range(1, nz // 2)
+    depth_spots = [z, *((z + s * k) % nz for k in steps for s in (-1, 1)), z + nz // 2]
+    depth_spots = [(at + nz) % nz * span for at in depth_spots]
+    row_spots = [0]
+    for k in range(1, nx):
+        row_spots += [(k * draws + c) * tokens, (k * draws + 1 - c) * tokens]
+    out_spots = [(x + k) % nx for k in (0, nx - 1, 1, 2)]
+    out_spots = [at // nc * (4 * draws) + at % nc * draws for at in out_spots]
+    limit = jnp.minimum(columns - x * WIDTH, WIDTH)
+    place = jnp.stack(
+        [
+            jnp.asarray(at, jnp.int32)
+            for at in (*depth_spots, *depth_spots, *row_spots, limit, *out_spots)
+        ]
+    )
     first_column = (y * nc + c) * columns + x * WIDTH
     wanted = (
         targets[:, None]
         - first_column
         - lax.broadcasted_iota(jnp.int32, (tokens, LANES), 1)
     )
-    limit = jnp.minimum(columns - x * WIDTH, WIDTH).astype(jnp.int32)
-    stats = local_stats(
-        depth_pieces[0] + depth_pieces[1], row_blocks, spots, wanted, limit
-    ).reshape(nc, 4 * draws, tokens)
-
-    sent = jnp.stack(
-        [
-            jnp.concatenate([stats[:, :, at : at + LANES], stats[:, :, TRAIN:]], axis=-1)
-            for at in range(0, TRAIN, LANES)
-        ]
-    )
-    sent = jnp.broadcast_to(
-        sent[:, None], (len(sent), nx // len(sent) * ny, *sent.shape[1:])
-    )
-    sent = sent.reshape(nx * ny * nc, *sent.shape[3:])
+    each = TRAIN // (nx * nz)
+    mine_at = ((x * nz + z) * each % LANES).astype(jnp.uint32)
+    own, place, wanted, mine_at = lax.optimization_barrier(
+        (own, place, wanted, mine_at)
+    )
+
+    depth_pieces = []
+    for half, part in enumerate(join_rows(own)):
+        depth_pieces.append(part)
+        up = down = part
+        for k in steps:
+            up = shift(up, "z", 1)
+            down = shift(down, "z", -1)
+            depth_pieces += [up, down]
+        far = (up, 1) if not half else (down, -1)
+        depth_pieces.append(shift(far[0], "z", far[1]))
+    left, right = shift(mine, "x", 1), shift(mine, "x", -1)
+    row_blocks = [[ordered]]
+    for rows in (left, right, shift(left, "x", 1)):
+        row_blocks.append([rows, shift(rows, "c", 1)])
+
+    sent = local_stats(depth_pieces, row_blocks, place, wanted, nx * ny * nc)
     got = lax.all_to_all(sent, ("x", "y", "c"), 0, 0, tiled=True)
     got = lax.all_to_all(
         join_stats(got, nz * nc), ("z", "c"), 0, 0, tiled=True
     )
     got = got.reshape(-1, got.shape[-1])
-    mine = lax.dynamic_slice_in_dim(got, at, each, 1)
+    mine = lax.dynamic_slice_in_dim(got, mine_at, each, 1)
     return covariance(mine, got[:, LANES:])
 
 

time: 136 us -> 146 us (1.074)
  blocking collectives: 20.4 us -> 28.9 us
  waiting for transfers between devices: 32.7 us -> 39 us
  starting transfers between devices: 41.9 us -> 39.1 us
  other arithmetic: 1.94 us -> 0.28 us
    all_to_all x0 -> x1, blocking collectives: none -> 11.6 us  [body(): got = lax.all_to_all(join_stats(got, nz * nc), ('z', 'c'), 0, 0, tiled=True)]
    all_to_all x1, waiting for transfers between devices: 5.49 us -> 16.3 us  [body(): own = lax.all_to_all(blocks, 'x', 0, 0, tiled=True)]
    all_to_all x1 -> x0, waiting for transfers between devices: 7.82 us -> none  [body(): got = lax.all_to_all(join_stats(got, nz * nc), ('z', 'c'), 0, 0, tiled=True)]
    all_to_all x1 -> x0, starting transfers between devices: 3.46 us -> none  [body(): got = lax.all_to_all(join_stats(got, nz * nc), ('z', 'c'), 0, 0, tiled=True)]
    ppermute x20, waiting for transfers between devices: 19.4 us -> 22.8 us  [shift(): return lax.ppermute(x, axis, [(i, (i + by) % size) for i in range(size)])]
    all_to_all x1, blocking collectives: 20.4 us -> 17.3 us  [body(): got = lax.all_to_all(sent, ('x', 'y', 'c'), 0, 0, tiled=True)]
    pallas_call x0 -> x1, Pallas kernels: none -> 1.94 us  [cut_columns(): pl.pallas_call(kernel, out_shape=jax.ShapeDtypeStruct((count, rows, WIDTH...]
    another operation x2 -> x1, local copies, waits for them, and re-layouts: 1.94 us -> 0.11 us  [body(): jnp.stack([jnp.asarray(at, jnp.int32) for at in (*depth_spots, *depth_spo...]
  transfers between devices with their start and end apart: 22 -> 21, of which waited for: 10 -> 9; matrix products, arithmetic and copies ran while one was open for 2% -> 0% of each run, Pallas kernels for 2% -> 3%
where the time goes in v3:
time: 146 us; the launch traced here: 145 us
  starting transfers between devices  39.1 us (27%)
  waiting for transfers between devices  39 us (27%)
  Pallas kernels  30.3 us (21%)
  blocking collectives  28.9 us (20%)
  local copies, waits for them, and re-layouts  4.3 us (3%)
  matrix products  2.66 us (2%)
    ppermute x20, starting transfers between devices, shift(): return lax.ppermute(x, axis, [(i, (i + by) % size) for i in range(size)])  35 us
    pallas_call x1, Pallas kernels, local_stats(): pl.pallas_call(functools.partial(loss_kernel, sizes=sizes, counts=counts)...  24.6 us
    ppermute x20, waiting for transfers between devices, shift(): return lax.ppermute(x, axis, [(i, (i + by) % size) for i in range(size)])  22.8 us
    all_to_all x1, blocking collectives, body(): got = lax.all_to_all(sent, ('x', 'y', 'c'), 0, 0, tiled=True)  17.3 us
    all_to_all x1, waiting for transfers between devices, body(): own = lax.all_to_all(blocks, 'x', 0, 0, tiled=True)  16.3 us
    all_to_all x1, blocking collectives, body(): got = lax.all_to_all(join_stats(got, nz * nc), ('z', 'c'), 0, 0, tiled=True)  11.6 us
    all_to_all x1, starting transfers between devices, body(): own = lax.all_to_all(blocks, 'x', 0, 0, tiled=True)  4.15 us
    unnamed x8, local copies, waits for them, and re-layouts  3.22 us
  transfers between devices with their start and end apart: 21, of which 9 were waited for; matrix products, arithmetic and copies ran while one was open for 0% of the time, Pallas kernels for 3%

profile of v3, /device:TPU:1, one launch (start us, length us, event | category | flops | bytes accessed | tf_op | source)
XLA Modules:
  0.0 145.1 jit_solution(11055116370697292597)
XLA Ops:
  1.3 1.8 %fusion.1 = bf16[896,768]{0,1:T(8,128)(2,1)S(1)} fusion(bf16[768,896]{1,0:T(8,128)(2,1)S(1)} %bitcast.24, s32[896]{0:T(1024)S(1)} %fusion.17), kind=kOutput, calls=%fused_computation.2 | convolution fusion | flops 1234616320 | bytes 2756096 | tf_op jit(solution)/shard_map/dot_general | solution.py:292
  4.1 2.0 %collective-permute-start.14 = (bf16[384,896]{1,0:T(8,128)(2,1)}, bf16[384,896]{1,0:T(8,128)(2,1)}, u32[]{:S(2)}, u32[]{:S(2)}) collective-permute-start(bf16[384,896]{1,0:T(8,128)(2,1)} %dynamic-slice_bitcast_fusion), channel_id=1, source_target_pairs={{0,64},{64,128},{128,192},{192,0},{1,65},{65,129},{129,193},{193,1... | collective-permute-start | bytes 2064392 | tf_op jit(solution)/shard_map/ppermute | solution.py:21
  7.4 1.9 %shard_map.37 = bf16[4,28,2432]{2,1,0:T(8,128)(2,1)} custom-call(bf16[28,9504]{1,0:T(8,128)(2,1)} %in_ref.1), custom_call_target="tpu_custom_call" | custom-call | tf_op jit(solution)/shard_map/pallas_call | solution.py:155
  9.3 4.2 %all-to-all-start = ((bf16[4,28,2432]{2,1,0:T(8,128)(2,1)}), bf16[4,28,2432]{2,1,0:T(8,128)(2,1)}, u32[]{:S(2)}, u32[]{:S(2)}) async-start(bf16[4,28,2432]{2,1,0:T(8,128)(2,1)} %shard_map.37), calls=%async_computation | async-start | bytes 1245184 | tf_op jit(solution)/shard_map/all_to_all | solution.py:283
  14.1 16.3 %all-to-all-done.in_ref = bf16[4,28,2432]{2,1,0:T(8,128)(2,1)} async-done(((bf16[4,28,2432]{2,1,0:T(8,128)(2,1)}), bf16[4,28,2432]{2,1,0:T(8,128)(2,1)}, u32[]{:S(2)}, u32[]{:S(2)}) %all-to-all-start) | async-done | bytes 544800 | tf_op jit(solution)/shard_map/all_to_all | solution.py:283
  30.4 2.1 %shard_map.38 = (bf16[112,1280]{1,0:T(8,128)(2,1)}, bf16[112,1152]{1,0:T(8,128)(2,1)}) custom-call(bf16[4,28,2432]{2,1,0:T(8,128)(2,1)} %all-to-all-done.in_ref), custom_call_target="tpu_custom_call" | custom-call | tf_op jit(solution)/shard_map/pallas_call | solution.py:191
  32.5 5.6 %collective-permute-start.8 = (bf16[112,1152]{1,0:T(8,128)(2,1)}, bf16[112,1152]{1,0:T(8,128)(2,1)S(1)}, u32[]{:S(2)}, u32[]{:S(2)}) collective-permute-start(bf16[112,1152]{1,0:T(8,128)(2,1)} %get-tuple-element.15.refs_8_), channel_id=1, source_target_pairs={{0,56},{8,0},{16,8},{24,16},{32,24},{40,32},{48,40},{56,48},{1,57}... | collective-permute-start | bytes 774152 | tf_op jit(solution)/shard_map/ppermute | solution.py:21
  38.7 2.7 %collective-permute-start.1 = (bf16[112,1280]{1,0:T(8,128)(2,1)}, bf16[112,1280]{1,0:T(8,128)(2,1)S(1)}, u32[]{:S(2)}, u32[]{:S(2)}) collective-permute-start(bf16[112,1280]{1,0:T(8,128)(2,1)} %get-tuple-element.14.refs_0_), channel_id=1, source_target_pairs={{0,56},{8,0},{16,8},{24,16},{32,24},{40,32},{48,40},{56,48},{1,57}... | collective-permute-start | bytes 860168 | tf_op jit(solution)/shard_map/ppermute | solution.py:21
  42.5 3.1 %collective-permute-done.7.refs_9_ = bf16[112,1152]{1,0:T(8,128)(2,1)S(1)} collective-permute-done((bf16[112,1152]{1,0:T(8,128)(2,1)}, bf16[112,1152]{1,0:T(8,128)(2,1)S(1)}, u32[]{:S(2)}, u32[]{:S(2)}) %collective-permute-start.7) | collective-permute-done | bytes 258080 | tf_op jit(solution)/shard_map/ppermute | solution.py:21
  48.6 3.3 %collective-permute-start.3 = (bf16[112,1280]{1,0:T(8,128)(2,1)S(1)}, bf16[112,1280]{1,0:T(8,128)(2,1)S(1)}, u32[]{:S(2)}, u32[]{:S(2)}) collective-permute-start(bf16[112,1280]{1,0:T(8,128)(2,1)S(1)} %collective-permute-done.1.refs_2_), channel_id=1, source_target_pairs={{0,56},{8,0},{16,8},{24,16},{32,24},{40,32},{48,40},{56,48},{1,57}... | collective-permute-start | bytes 860168 | tf_op jit(solution)/shard_map/ppermute | solution.py:21
  51.9 2.1 %collective-permute-done.10.refs_12_ = bf16[112,1152]{1,0:T(8,128)(2,1)S(1)} collective-permute-done((bf16[112,1152]{1,0:T(8,128)(2,1)S(1)}, bf16[112,1152]{1,0:T(8,128)(2,1)S(1)}, u32[]{:S(2)}, u32[]{:S(2)}) %collective-permute-start.10) | collective-permute-done | bytes 258080 | tf_op jit(solution)/shard_map/ppermute | solution.py:21
  54.0 3.4 %collective-permute-start.12 = (bf16[112,1152]{1,0:T(8,128)(2,1)S(1)}, bf16[112,1152]{1,0:T(8,128)(2,1)S(1)}, u32[]{:S(2)}, u32[]{:S(2)}) collective-permute-start(bf16[112,1152]{1,0:T(8,128)(2,1)S(1)} %collective-permute-done.10.refs_12_), channel_id=1, source_target_pairs={{0,56},{8,0},{16,8},{24,16},{32,24},{40,32},{48,40},{56,48},{1,57}... | collective-permute-start | bytes 774152 | tf_op jit(solution)/shard_map/ppermute | solution.py:21
  57.5 2.7 %collective-permute-done.3.refs_4_ = bf16[112,1280]{1,0:T(8,128)(2,1)S(1)} collective-permute-done((bf16[112,1280]{1,0:T(8,128)(2,1)S(1)}, bf16[112,1280]{1,0:T(8,128)(2,1)S(1)}, u32[]{:S(2)}, u32[]{:S(2)}) %collective-permute-start.3) | collective-permute-done | bytes 286752 | tf_op jit(solution)/shard_map/ppermute | solution.py:21
  60.2 4.4 %collective-permute-start.17 = (bf16[384,896]{1,0:T(8,128)(2,1)}, bf16[384,896]{1,0:T(8,128)(2,1)S(1)}, u32[]{:S(2)}, u32[]{:S(2)}) collective-permute-start(bf16[384,896]{1,0:T(8,128)(2,1)} %collective-permute-done.16.refs_19_), channel_id=1, source_target_pairs={{0,1},{1,0},{2,3},{3,2},{4,5},{5,4},{6,7},{7,6},{8,9},{9,8},{10,11... | collective-permute-start | bytes 2064392 | tf_op jit(solution)/shard_map/ppermute | solution.py:21
  64.6 4.8 %collective-permute-start.15 = (bf16[384,896]{1,0:T(8,128)(2,1)}, bf16[384,896]{1,0:T(8,128)(2,1)S(1)}, u32[]{:S(2)}, u32[]{:S(2)}) collective-permute-start(bf16[384,896]{1,0:T(8,128)(2,1)} %collective-permute-done.14.refs_17_), channel_id=1, source_target_pairs={{0,1},{1,0},{2,3},{3,2},{4,5},{5,4},{6,7},{7,6},{8,9},{9,8},{10,11... | collective-permute-start | bytes 2064392 | tf_op jit(solution)/shard_map/ppermute | solution.py:21
  69.5 2.7 %collective-permute-start.5 = (bf16[112,1280]{1,0:T(8,128)(2,1)S(1)}, bf16[112,1280]{1,0:T(8,128)(2,1)S(1)}, u32[]{:S(2)}, u32[]{:S(2)}) collective-permute-start(bf16[112,1280]{1,0:T(8,128)(2,1)S(1)} %collective-permute-done.3.refs_4_), channel_id=1, source_target_pairs={{0,56},{8,0},{16,8},{24,16},{32,24},{40,32},{48,40},{56,48},{1,57}... | collective-permute-start | bytes 860168 | tf_op jit(solution)/shard_map/ppermute | solution.py:21
  72.2 6.5 %collective-permute-done.4.refs_5_ = bf16[112,1280]{1,0:T(8,128)(2,1)S(1)} collective-permute-done((bf16[112,1280]{1,0:T(8,128)(2,1)S(1)}, bf16[112,1280]{1,0:T(8,128)(2,1)S(1)}, u32[]{:S(2)}, u32[]{:S(2)}) %collective-permute-start.4) | collective-permute-done | bytes 286752 | tf_op jit(solution)/shard_map/ppermute | solution.py:21
  78.7 2.7 %collective-permute-start.13 = (bf16[112,1152]{1,0:T(8,128)(2,1)S(1)}, bf16[112,1152]{1,0:T(8,128)(2,1)S(1)}, u32[]{:S(2)}, u32[]{:S(2)}) collective-permute-start(bf16[112,1152]{1,0:T(8,128)(2,1)S(1)} %collective-permute-done.12.refs_14_), channel_id=1, source_target_pairs={{0,56},{8,0},{16,8},{24,16},{32,24},{40,32},{48,40},{56,48},{1,57}... | collective-permute-start | bytes 774152 | tf_op jit(solution)/shard_map/ppermute | solution.py:21
  81.3 4.0 %collective-permute-done.13.refs_15_ = bf16[112,1152]{1,0:T(8,128)(2,1)S(1)} collective-permute-done((bf16[112,1152]{1,0:T(8,128)(2,1)S(1)}, bf16[112,1152]{1,0:T(8,128)(2,1)S(1)}, u32[]{:S(2)}, u32[]{:S(2)}) %collective-permute-start.13) | collective-permute-done | bytes 258080 | tf_op jit(solution)/shard_map/ppermute | solution.py:21
  85.4 1.6 %collective-permute-done.6.refs_7_ = bf16[112,1280]{1,0:T(8,128)(2,1)S(1)} collective-permute-done((bf16[112,1280]{1,0:T(8,128)(2,1)S(1)}, bf16[112,1280]{1,0:T(8,128)(2,1)S(1)}, u32[]{:S(2)}, u32[]{:S(2)}) %collective-permute-start.6) | collective-permute-done | bytes 286752 | tf_op jit(solution)/shard_map/ppermute | solution.py:21
  88.9 24.6 %shard_map.39 = f32[32,8,256]{2,1,0:T(8,128)S(1)} custom-call(s32[28]{0:T(128)S(1)} %stack.87.place_ref, s32[384,128]{1,0:T(8,128)S(1)} %iota_subtract_fusion.wanted_ref, bf16[112,1280]{1,0:T(8,128)(2,1)S(1)} %copy-done.1, bf16[112,1280]{1,0:T(8,128)(2,1)S(1)} %collective-permute-done.refs_1_, bf16[112,1280]{1,0:T(8,128)(2,1)S(1)} %collective-permute-done.1.refs_2_, ...), custom_call_target="tpu_custom_call" | custom-call | flops 13388218368 | bytes 9863168 | tf_op jit(solution)/shard_map/pallas_call | solution.py:232
  113.5 17.3 %all_to_all.15.in_ref = f32[32,8,256]{2,1,0:T(8,128)} all-to-all(f32[32,8,256]{2,1,0:T(8,128)S(1)} %shard_map.39), channel_id=1, replica_groups=mesh['x'=4,'z'=8,'y'=4,'c'=2] {'x','y','c'}, dimensions={0} | all-to-all | bytes 524288 | tf_op jit(solution)/shard_map/all_to_all | solution.py:342
  130.8 1.7 %shard_map.40 = f32[16,4,256]{2,1,0:T(4,128)} custom-call(f32[32,8,256]{2,1,0:T(8,128)} %all_to_all.15.in_ref), custom_call_target="tpu_custom_call" | custom-call | tf_op jit(solution)/shard_map/pallas_call | solution.py:212
  132.4 11.6 %all_to_all.16 = f32[16,4,256]{2,1,0:T(4,128)S(1)} all-to-all(f32[16,4,256]{2,1,0:T(4,128)} %shard_map.40), channel_id=1, replica_groups=mesh['x'=4,'z'=8,'y'=4,'c'=2] {'z','c'}, dimensions={0} | all-to-all | bytes 131072 | tf_op jit(solution)/shard_map/all_to_all | solution.py:343
  (44 shorter events, 11.6 us)
Async XLA Ops:
  0.0 1.3 copy-start
  4.1 9.9 %copy-start.3 = (s32[384]{0:T(512)S(1)}, s32[384]{0:T(512)}, u32[]{:S(2)}) copy-start(s32[384]{0:T(512)} %param.5) | copy-start | bytes 4612
  4.1 34.0 %collective-permute-start.14 = (bf16[384,896]{1,0:T(8,128)(2,1)}, bf16[384,896]{1,0:T(8,128)(2,1)}, u32[]{:S(2)}, u32[]{:S(2)}) collective-permute-start(bf16[384,896]{1,0:T(8,128)(2,1)} %dynamic-slice_bitcast_fusion), channel_id=1, source_target_pairs={{0,64},{64,128},{128,192},{192,0},{1,65},{65,129},{129,193},{193,1... | collective-permute-start | bytes 2064392 | tf_op jit(solution)/shard_map/ppermute | solution.py:21
  6.1 39.7 %collective-permute-start.16 = (bf16[384,896]{1,0:T(8,128)(2,1)}, bf16[384,896]{1,0:T(8,128)(2,1)}, u32[]{:S(2)}, u32[]{:S(2)}) collective-permute-start(bf16[384,896]{1,0:T(8,128)(2,1)} %dynamic-slice_bitcast_fusion), channel_id=1, source_target_pairs={{0,192},{64,0},{128,64},{192,128},{1,193},{65,1},{129,65},{193,129... | collective-permute-start | bytes 2064392 | tf_op jit(solution)/shard_map/ppermute | solution.py:21
  9.3 21.1 %all-to-all-start = ((bf16[4,28,2432]{2,1,0:T(8,128)(2,1)}), bf16[4,28,2432]{2,1,0:T(8,128)(2,1)}, u32[]{:S(2)}, u32[]{:S(2)}) async-start(bf16[4,28,2432]{2,1,0:T(8,128)(2,1)} %shard_map.37), calls=%async_computation | async-start | bytes 1245184 | tf_op jit(solution)/shard_map/all_to_all | solution.py:283
  32.5 9.9 %collective-permute-start.8 = (bf16[112,1152]{1,0:T(8,128)(2,1)}, bf16[112,1152]{1,0:T(8,128)(2,1)S(1)}, u32[]{:S(2)}, u32[]{:S(2)}) collective-permute-start(bf16[112,1152]{1,0:T(8,128)(2,1)} %get-tuple-element.15.refs_8_), channel_id=1, source_target_pairs={{0,56},{8,0},{16,8},{24,16},{32,24},{40,32},{48,40},{56,48},{1,57}... | collective-permute-start | bytes 774152 | tf_op jit(solution)/shard_map/ppermute | solution.py:21
  38.1 31.3 %collective-permute-start.18 = (bf16[384,896]{1,0:T(8,128)(2,1)}, bf16[384,896]{1,0:T(8,128)(2,1)S(1)}, u32[]{:S(2)}, u32[]{:S(2)}) collective-permute-start(bf16[384,896]{1,0:T(8,128)(2,1)} %collective-permute-done.14.refs_17_), channel_id=1, source_target_pairs={{0,64},{64,128},{128,192},{192,0},{1,65},{65,129},{129,193},{193,1... | collective-permute-start | bytes 2064392 | tf_op jit(solution)/shard_map/ppermute | solution.py:21
  38.7 6.9 %collective-permute-start.7 = (bf16[112,1152]{1,0:T(8,128)(2,1)}, bf16[112,1152]{1,0:T(8,128)(2,1)S(1)}, u32[]{:S(2)}, u32[]{:S(2)}) collective-permute-start(bf16[112,1152]{1,0:T(8,128)(2,1)} %get-tuple-element.15.refs_8_), channel_id=1, source_target_pairs={{0,8},{8,16},{16,24},{24,32},{32,40},{40,48},{48,56},{56,0},{1,9},... | collective-permute-start | bytes 774152 | tf_op jit(solution)/shard_map/ppermute | solution.py:21
  38.7 9.9 %collective-permute-start.1 = (bf16[112,1280]{1,0:T(8,128)(2,1)}, bf16[112,1280]{1,0:T(8,128)(2,1)S(1)}, u32[]{:S(2)}, u32[]{:S(2)}) collective-permute-start(bf16[112,1280]{1,0:T(8,128)(2,1)} %get-tuple-element.14.refs_0_), channel_id=1, source_target_pairs={{0,56},{8,0},{16,8},{24,16},{32,24},{40,32},{48,40},{56,48},{1,57}... | collective-permute-start | bytes 860168 | tf_op jit(solution)/shard_map/ppermute | solution.py:21
  42.5 9.5 %collective-permute-start = (bf16[112,1280]{1,0:T(8,128)(2,1)}, bf16[112,1280]{1,0:T(8,128)(2,1)S(1)}, u32[]{:S(2)}, u32[]{:S(2)}) collective-permute-start(bf16[112,1280]{1,0:T(8,128)(2,1)} %get-tuple-element.14.refs_0_), channel_id=1, source_target_pairs={{0,8},{8,16},{16,24},{24,32},{32,40},{40,48},{48,56},{56,0},{1,9},... | collective-permute-start | bytes 860168 | tf_op jit(solution)/shard_map/ppermute | solution.py:21
  45.6 8.4 %collective-permute-start.10 = (bf16[112,1152]{1,0:T(8,128)(2,1)S(1)}, bf16[112,1152]{1,0:T(8,128)(2,1)S(1)}, u32[]{:S(2)}, u32[]{:S(2)}) collective-permute-start(bf16[112,1152]{1,0:T(8,128)(2,1)S(1)} %collective-permute-done.8.refs_10_), channel_id=1, source_target_pairs={{0,56},{8,0},{16,8},{24,16},{32,24},{40,32},{48,40},{56,48},{1,57}... | collective-permute-start | bytes 774152 | tf_op jit(solution)/shard_map/ppermute | solution.py:21
  45.8 11.7 %collective-permute-start.9 = (bf16[112,1152]{1,0:T(8,128)(2,1)S(1)}, bf16[112,1152]{1,0:T(8,128)(2,1)S(1)}, u32[]{:S(2)}, u32[]{:S(2)}) collective-permute-start(bf16[112,1152]{1,0:T(8,128)(2,1)S(1)} %collective-permute-done.7.refs_9_), channel_id=1, source_target_pairs={{0,8},{8,16},{16,24},{24,32},{32,40},{40,48},{48,56},{56,0},{1,9},... | collective-permute-start | bytes 774152 | tf_op jit(solution)/shard_map/ppermute | solution.py:21
  48.6 11.6 %collective-permute-start.3 = (bf16[112,1280]{1,0:T(8,128)(2,1)S(1)}, bf16[112,1280]{1,0:T(8,128)(2,1)S(1)}, u32[]{:S(2)}, u32[]{:S(2)}) collective-permute-start(bf16[112,1280]{1,0:T(8,128)(2,1)S(1)} %collective-permute-done.1.refs_2_), channel_id=1, source_target_pairs={{0,56},{8,0},{16,8},{24,16},{32,24},{40,32},{48,40},{56,48},{1,57}... | collective-permute-start | bytes 860168 | tf_op jit(solution)/shard_map/ppermute | solution.py:21
  51.9 12.6 %collective-permute-start.2 = (bf16[112,1280]{1,0:T(8,128)(2,1)S(1)}, bf16[112,1280]{1,0:T(8,128)(2,1)S(1)}, u32[]{:S(2)}, u32[]{:S(2)}) collective-permute-start(bf16[112,1280]{1,0:T(8,128)(2,1)S(1)} %collective-permute-done.refs_1_), channel_id=1, source_target_pairs={{0,8},{8,16},{16,24},{24,32},{32,40},{40,48},{48,56},{56,0},{1,9},... | collective-permute-start | bytes 860168 | tf_op jit(solution)/shard_map/ppermute | solution.py:21
  54.0 15.4 %collective-permute-start.12 = (bf16[112,1152]{1,0:T(8,128)(2,1)S(1)}, bf16[112,1152]{1,0:T(8,128)(2,1)S(1)}, u32[]{:S(2)}, u32[]{:S(2)}) collective-permute-start(bf16[112,1152]{1,0:T(8,128)(2,1)S(1)} %collective-permute-done.10.refs_12_), channel_id=1, source_target_pairs={{0,56},{8,0},{16,8},{24,16},{32,24},{40,32},{48,40},{56,48},{1,57}... | collective-permute-start | bytes 774152 | tf_op jit(solution)/shard_map/ppermute | solution.py:21
  57.5 12.1 %collective-permute-start.11 = (bf16[112,1152]{1,0:T(8,128)(2,1)S(1)}, bf16[112,1152]{1,0:T(8,128)(2,1)S(1)}, u32[]{:S(2)}, u32[]{:S(2)}) collective-permute-start(bf16[112,1152]{1,0:T(8,128)(2,1)S(1)} %collective-permute-done.9.refs_11_), channel_id=1, source_target_pairs={{0,8},{8,16},{16,24},{24,32},{32,40},{40,48},{48,56},{56,0},{1,9},... | collective-permute-start | bytes 774152 | tf_op jit(solution)/shard_map/ppermute | solution.py:21
  60.2 21.2 %collective-permute-start.17 = (bf16[384,896]{1,0:T(8,128)(2,1)}, bf16[384,896]{1,0:T(8,128)(2,1)S(1)}, u32[]{:S(2)}, u32[]{:S(2)}) collective-permute-start(bf16[384,896]{1,0:T(8,128)(2,1)} %collective-permute-done.16.refs_19_), channel_id=1, source_target_pairs={{0,1},{1,0},{2,3},{3,2},{4,5},{5,4},{6,7},{7,6},{8,9},{9,8},{10,11... | collective-permute-start | bytes 2064392 | tf_op jit(solution)/shard_map/ppermute | solution.py:21
  64.6 16.8 %collective-permute-start.15 = (bf16[384,896]{1,0:T(8,128)(2,1)}, bf16[384,896]{1,0:T(8,128)(2,1)S(1)}, u32[]{:S(2)}, u32[]{:S(2)}) collective-permute-start(bf16[384,896]{1,0:T(8,128)(2,1)} %collective-permute-done.14.refs_17_), channel_id=1, source_target_pairs={{0,1},{1,0},{2,3},{3,2},{4,5},{5,4},{6,7},{7,6},{8,9},{9,8},{10,11... | collective-permute-start | bytes 2064392 | tf_op jit(solution)/shard_map/ppermute | solution.py:21
  69.4 17.6 %collective-permute-start.19 = (bf16[384,896]{1,0:T(8,128)(2,1)S(1)}, bf16[384,896]{1,0:T(8,128)(2,1)S(1)}, u32[]{:S(2)}, u32[]{:S(2)}) collective-permute-start(bf16[384,896]{1,0:T(8,128)(2,1)S(1)} %collective-permute-done.18.refs_21_), channel_id=1, source_target_pairs={{0,1},{1,0},{2,3},{3,2},{4,5},{5,4},{6,7},{7,6},{8,9},{9,8},{10,11... | collective-permute-start | bytes 2064392 | tf_op jit(solution)/shard_map/ppermute | solution.py:21
  69.4 9.3 %collective-permute-start.4 = (bf16[112,1280]{1,0:T(8,128)(2,1)S(1)}, bf16[112,1280]{1,0:T(8,128)(2,1)S(1)}, u32[]{:S(2)}, u32[]{:S(2)}) collective-permute-start(bf16[112,1280]{1,0:T(8,128)(2,1)S(1)} %collective-permute-done.2.refs_3_), channel_id=1, source_target_pairs={{0,8},{8,16},{16,24},{24,32},{32,40},{40,48},{48,56},{56,0},{1,9},... | collective-permute-start | bytes 860168 | tf_op jit(solution)/shard_map/ppermute | solution.py:21
  69.5 9.2 %collective-permute-start.5 = (bf16[112,1280]{1,0:T(8,128)(2,1)S(1)}, bf16[112,1280]{1,0:T(8,128)(2,1)S(1)}, u32[]{:S(2)}, u32[]{:S(2)}) collective-permute-start(bf16[112,1280]{1,0:T(8,128)(2,1)S(1)} %collective-permute-done.3.refs_4_), channel_id=1, source_target_pairs={{0,56},{8,0},{16,8},{24,16},{32,24},{40,32},{48,40},{56,48},{1,57}... | collective-permute-start | bytes 860168 | tf_op jit(solution)/shard_map/ppermute | solution.py:21
  78.7 8.3 %collective-permute-start.6 = (bf16[112,1280]{1,0:T(8,128)(2,1)S(1)}, bf16[112,1280]{1,0:T(8,128)(2,1)S(1)}, u32[]{:S(2)}, u32[]{:S(2)}) collective-permute-start(bf16[112,1280]{1,0:T(8,128)(2,1)S(1)} %collective-permute-done.4.refs_5_), channel_id=1, source_target_pairs={{0,8},{8,16},{16,24},{24,32},{32,40},{40,48},{48,56},{56,0},{1,9},... | collective-permute-start | bytes 860168 | tf_op jit(solution)/shard_map/ppermute | solution.py:21
  78.7 6.7 %collective-permute-start.13 = (bf16[112,1152]{1,0:T(8,128)(2,1)S(1)}, bf16[112,1152]{1,0:T(8,128)(2,1)S(1)}, u32[]{:S(2)}, u32[]{:S(2)}) collective-permute-start(bf16[112,1152]{1,0:T(8,128)(2,1)S(1)} %collective-permute-done.12.refs_14_), channel_id=1, source_target_pairs={{0,56},{8,0},{16,8},{24,16},{32,24},{40,32},{48,40},{56,48},{1,57}... | collective-permute-start | bytes 774152 | tf_op jit(solution)/shard_map/ppermute | solution.py:21
  87.0 1.0 copy-start.1
  (1 other events, 0.9 us)
